TPU v7x, 256 devices: a whole 4x4x8 slice. The times are simulated.
256 devices in a mesh: dp: 32 (over z_hi, x, core), ctx: 8 (over y, z_lo).
Axes of the slice: x: 4, y: 4, z: 8 (z_hi: 4, z_lo: 2; z = z_hi * 2 + z_lo), core: 2. Of those that a mesh axis runs over, the one named last changes fastest.
Arguments:
- clip_in: bfloat16 [32, 32, 4, 96, 128], P('dp', 'ctx'), may hold values from -100 to 100
- norm_gain: float32 [128], replicated, may hold values from 0.1 to 1.9
- norm_bias: float32 [128], replicated, may hold values from -3 to 3
- conv_weight: bfloat16 [3456, 256], replicated, may hold values from -0.109375 to 0.109375
- short_weight: bfloat16 [128, 256], replicated, may hold values from -0.5 to 0.5
- out_cotangent: bfloat16 [32, 32, 4, 96, 256], P('dp', 'ctx'), may hold values from -6 to 6
Outputs:
- clip_out: bfloat16 [32, 32, 4, 96, 256], P('dp', 'ctx')
- clip_grad: bfloat16 [32, 32, 4, 96, 128], P('dp', 'ctx')
- conv_grad: float32 [3456, 256], P('dp', 'ctx')
- short_grad: float32 [128, 256], P('dp', 'ctx')
All inputs are finite; a program needn't handle non-finite values.
Results may differ from a plain program's by a relative error of at most 0.0027.
Values may be sent and summed in bfloat16 or wider, within the bound.
A program may use at most 128 MiB of HBM per device.

v0:
```python
import jax
import jax.numpy as jnp
from jax import lax
from jax.sharding import PartitionSpec as P

GROUPS = 32
KT = 3
KS = 3


epsilon = 1e-06


def from_behind(value, axis, steps):
    count = lax.axis_size(axis)
    initial, last = (max(0, -steps), min(count, count - steps))
    return lax.ppermute(value, axis, [(source, source + steps) for source in range(initial, last)])


def group_stats(clip_in, members):
    batch_clips = clip_in.shape[0]
    in_width = clip_in.shape[4]
    per_group = in_width // GROUPS
    widened = clip_in.astype(jnp.float32).reshape(clip_in.shape[:4] + (GROUPS, per_group))
    totals = lax.psum(
        (jnp.sum(widened, axis=(1, 2, 3, 5)), jnp.sum(widened * widened, axis=(1, 2, 3, 5))), "ctx"
    )
    group_mean = totals[0] / members
    variance = totals[1] / members - group_mean * group_mean
    inv_std = lax.rsqrt(variance + epsilon)
    mean_chan = jnp.repeat(group_mean, per_group, axis=1).reshape(batch_clips, 1, 1, 1, in_width)
    inv_chan = jnp.repeat(inv_std, per_group, axis=1).reshape(batch_clips, 1, 1, 1, in_width)
    return (mean_chan, inv_chan)


def body(clip_in, norm_gain, norm_bias, conv_weight, short_weight, out_cotangent):
    batch_clips, frames, height, breadth, in_width = clip_in.shape
    out_width = conv_weight.shape[1]
    per_group = in_width // GROUPS
    ctx_size = lax.axis_size("ctx")
    total_frames = frames * ctx_size
    members = total_frames * height * breadth * per_group
    at_start = lax.axis_index("ctx") == 0
    mean_chan, inv_chan = group_stats(clip_in, members)
    standard = (clip_in.astype(jnp.float32) - mean_chan) * inv_chan
    standard, affine = (standard, standard * norm_gain + norm_bias)
    hidden = jax.nn.silu(affine).astype(jnp.bfloat16)
    prev_hidden = from_behind(hidden[:, frames - 2 :], "ctx", 1)
    repeated = jnp.concatenate([hidden[:, :1], hidden[:, :1]], axis=1)
    front = jnp.where(at_start, repeated, prev_hidden)
    padded = jnp.concatenate([front, hidden], axis=1)
    padded = jnp.pad(padded, ((0, 0), (0, 0), (1, 1), (1, 1), (0, 0)))
    pieces = []
    for tap_t in range(KT):
        for tap_r in range(KS):
            for tap_c in range(KS):
                pieces.append(
                    padded[
                        :, tap_t : tap_t + frames, tap_r : tap_r + height, tap_c : tap_c + breadth
                    ]
                )
    columns = jnp.concatenate(pieces, axis=-1).reshape(-1, KT * KS * KS * in_width)
    in_flat = clip_in.reshape(-1, in_width)
    result = jnp.dot(columns, conv_weight, preferred_element_type=jnp.float32)
    result = result + jnp.dot(in_flat, short_weight, preferred_element_type=jnp.float32)
    clip_out = result.astype(jnp.bfloat16).reshape(batch_clips, frames, height, breadth, out_width)
    following = from_behind(out_cotangent[:, :2], "ctx", -1)
    extended = jnp.concatenate([out_cotangent, following], axis=1)
    padded_cot = jnp.pad(extended, ((0, 0), (0, 0), (1, 1), (1, 1), (0, 0)))
    spatial = []
    for tap_r in range(KS):
        for tap_c in range(KS):
            spatial.append(
                padded_cot[:, :, 2 - tap_r : 2 - tap_r + height, 2 - tap_c : 2 - tap_c + breadth]
            )
    spatial = jnp.concatenate(spatial, axis=-1)
    w_back = (
        conv_weight.reshape(KT, KS * KS, in_width, out_width)
        .transpose(0, 1, 3, 2)
        .reshape(KT, KS * KS * out_width, in_width)
    )
    grad_hidden = jnp.zeros((batch_clips * frames * height * breadth, in_width), jnp.float32)
    for tap_t in range(KT):
        block = spatial[:, 2 - tap_t : 2 - tap_t + frames].reshape(-1, KS * KS * out_width)
        grad_hidden = grad_hidden + jnp.dot(
            block, w_back[tap_t], preferred_element_type=jnp.float32
        )
    grad_hidden = grad_hidden.reshape(batch_clips, frames, height, breadth, in_width)

    def pad_terms():
        lead = spatial[:, 0].reshape(-1, KS * KS * out_width)
        second = spatial[:, 1].reshape(-1, KS * KS * out_width)
        terms = jnp.dot(lead, w_back[0], preferred_element_type=jnp.float32)
        terms = terms + jnp.dot(second, w_back[0], preferred_element_type=jnp.float32)
        terms = terms + jnp.dot(lead, w_back[1], preferred_element_type=jnp.float32)
        return terms.reshape(batch_clips, height, breadth, in_width)

    def no_terms():
        return jnp.zeros((batch_clips, height, breadth, in_width), jnp.float32)

    extra_terms = lax.cond(at_start, pad_terms, no_terms)
    grad_hidden = grad_hidden.at[:, 0].add(extra_terms)
    logistic = jax.nn.sigmoid(affine)
    grad_standard = grad_hidden * logistic * (1.0 + affine * (1.0 - logistic)) * norm_gain
    grouped_grad = grad_standard.reshape(grad_standard.shape[:4] + (GROUPS, per_group))
    grouped_std = standard.reshape(standard.shape[:4] + (GROUPS, per_group))
    grad_sums = lax.psum(
        (
            jnp.sum(grouped_grad, axis=(1, 2, 3, 5)),
            jnp.sum(grouped_grad * grouped_std, axis=(1, 2, 3, 5)),
        ),
        "ctx",
    )
    mean_grad = jnp.repeat(grad_sums[0] / members, per_group, axis=1).reshape(
        batch_clips, 1, 1, 1, in_width
    )
    mean_cross = jnp.repeat(grad_sums[1] / members, per_group, axis=1).reshape(
        batch_clips, 1, 1, 1, in_width
    )
    cot_flat = out_cotangent.reshape(-1, out_width)
    shortcut = lax.dot_general(
        cot_flat, short_weight, (((1,), (1,)), ((), ())), preferred_element_type=jnp.float32
    )
    in_grad = (grad_standard - mean_grad - standard * mean_cross) * inv_chan + shortcut.reshape(
        batch_clips, frames, height, breadth, in_width
    )
    clip_grad = in_grad.astype(jnp.bfloat16)
    conv_part = lax.dot_general(
        columns, cot_flat, (((0,), (0,)), ((), ())), preferred_element_type=jnp.float32
    )
    short_part = lax.dot_general(
        in_flat, cot_flat, (((0,), (0,)), ((), ())), preferred_element_type=jnp.float32
    )
    conv_part, short_part = (
        lax.psum_scatter(conv_part, "dp", scatter_dimension=0, tiled=True),
        lax.psum_scatter(short_part, "dp", scatter_dimension=0, tiled=True),
    )
    conv_part, short_part = (
        lax.psum_scatter(conv_part, "ctx", scatter_dimension=1, tiled=True),
        lax.psum_scatter(short_part, "ctx", scatter_dimension=1, tiled=True),
    )
    scale_factor = 1.0 / (batch_clips * lax.axis_size("dp") * total_frames)
    return (clip_out, clip_grad, conv_part * scale_factor, short_part * scale_factor)


def solution(mesh):
    return jax.shard_map(
        body,
        mesh=mesh,
        in_specs=(
            P("dp", "ctx", None, None, None),
            P(),
            P(),
            P(),
            P(),
            P("dp", "ctx", None, None, None),
        ),
        out_specs=(
            P("dp", "ctx", None, None, None),
            P("dp", "ctx", None, None, None),
            P("dp", "ctx"),
            P("dp", "ctx"),
        ),
        check_vma=False,
    )
```

profile of v0, /device:TPU:1, one launch (start us, length us, event | category | flops | bytes accessed | tf_op | source)
XLA Modules:
  0.0 555.3 jit_solution(3573810583214576862)
XLA Ops:
  7.2 2.3 convolution_bitcast_fusion.1
  10.6 1.3 collective-permute-start.1
  11.9 1.5 fusion.75
  15.1 1.3 fusion.76
  17.1 18.2 %all-reduce.6 = (f32[1,32]{1,0:T(1,128)S(1)}, f32[1,32]{1,0:T(1,128)S(1)}) all-reduce(f32[1,32]{1,0:T(1,128)S(1)} %bitcast.111, f32[1,32]{1,0:T(1,128)S(1)} %bitcast.110), channel_id=1, replica_groups=mesh['dp'=32,'ctx'=8] {'ctx'}, use_global_device_ids=true, to_apply=%region_5.6 | all-reduce | flops 64 | bytes 512 | tf_op jit(solution)/shard_map/psum | solution.py:25
  35.3 241.0 %all-reduce.9.cloned.1.call-done = f32[128,256]{1,0:T(8,128)} async-done(((f32[128,256]{1,0:T(8,128)}), f32[128,256]{1,0:T(8,128)}) %all-reduce.9.cloned.1.call-update) | async-done | bytes 131088
  282.1 31.7 %reduce-scatter.11.cloned.1.call-done = f32[32,4]{1,0:T(8,128)} async-done(((f32[256,4]{1,0:T(8,128)}), f32[32,4]{1,0:T(8,128)}) %reduce-scatter.11.cloned.1.call-update) | async-done | bytes 528
  315.8 1.5 slice_dynamic-update-slice_fusion.7
  317.4 1.6 slice_dynamic-update-slice_fusion.6
  320.2 1.6 slice_dynamic-update-slice_fusion.4
  324.9 1.7 slice_dynamic-update-slice_fusion.2
  326.5 1.6 slice_dynamic-update-slice_fusion.1
  329.4 14.0 %fusion.74 = (bf16[1,4,4,96,2304]{4,3,2,1,0:T(8,128)(2,1)}, bf16[1,4,4,96,2304]{4,3,2,1,0:T(8,128)(2,1)}, bf16[1,4,4,96,2304]{4,3,2,1,0:T(8,128)(2,1)S(1)}) fusion(bf16[1,6,4,96,2304]{4,3,2,1,0:T(8,128)(2,1)} %slice_dynamic-update-slice_fusion), kind=kLoop, calls=%fused_computation.134 | loop fusion | bytes 42467328 | tf_op jit(solution)/shard_map/slice | solution.py:84
  343.4 2.9 fusion.79
  346.3 8.0 %conditional.1 = (f32[1,1,4,96,128]{4,3,2,1,0:T(8,128)S(1)}) conditional(s32[]{:T(128)} %convert_element_type.23, () %tuple.20, (bf16[1,6,4,96,2304]{4,3,2,1,0:T(8,128)(2,1)}, bf16[3,9,256,128]{2,3,1,0:T(8,128)(2,1)S(1)}) %tuple.51), branch_computations={%region_6.7_spmd, %region_7.8_spmd} | conditional | flops 679575552 | bytes 21037064 | solution.py:101
  346.3 2.3 copy.21
  348.6 1.3 fusion.73
  350.0 2.2 fusion.72
  354.3 5.4 convolution_add_fusion.4
  359.8 5.2 convolution_add_fusion.3
  365.1 1.4 fusion.70
  367.6 12.6 %all-reduce.5 = (f32[1,32]{1,0:T(1,128)S(1)}, f32[1,32]{1,0:T(1,128)S(1)}) all-reduce(f32[1,32]{1,0:T(1,128)S(1)} %bitcast.113, f32[1,32]{1,0:T(1,128)S(1)} %bitcast.112), channel_id=1, replica_groups=mesh['dp'=32,'ctx'=8] {'ctx'}, use_global_device_ids=true, to_apply=%region_13.14 | all-reduce | flops 64 | bytes 512 | tf_op jit(solution)/shard_map/psum | solution.py:107
  380.6 3.6 collective-permute-start
  384.2 2.2 fusion.16
  390.8 4.0 copy-done.5
  394.8 4.8 fusion.3
  399.6 95.1 %fusion = f32[112,256]{1,0:T(8,128)S(1)} fusion(f32[3456,256]{1,0:T(8,128)} %fusion.3), kind=kCustom, calls=%all-reduce-scatter | all-reduce-scatter fusion | flops 917505 | bytes 3654656
  494.7 1.9 collective-permute-start.2
  496.6 1.3 collective-permute-start.3
  497.9 8.2 %fusion.78 = f32[1536,256]{1,0:T(8,128)} fusion(bf16[1536,3456]{1,0:T(8,128)(2,1)} %bitcast.109, bf16[3456,256]{1,0:T(8,128)(2,1)S(1)} %copy-done.3), kind=kOutput, calls=%fused_computation.138 | convolution fusion | flops 2717908992 | bytes 13959168 | tf_op jit(solution)/shard_map/dot_general | solution.py:64
  507.3 2.6 fusion.9
  510.0 37.3 %reduce-scatter.9.cloned.1.call-done = f32[32,108]{1,0:T(8,128)} async-done(((f32[256,108]{1,0:T(8,128)}), f32[32,108]{1,0:T(8,128)}) %reduce-scatter.9.cloned.1.call-update) | async-done | bytes 13840
  (100 shorter events, 25.9 us)
Async XLA Ops:
  7.2 377.0 %copy-start = (bf16[128,256]{1,0:T(8,128)(2,1)S(1)}, bf16[128,256]{1,0:T(8,128)(2,1)}, u32[]{:S(2)}) copy-start(bf16[128,256]{1,0:T(8,128)(2,1)} %param.14) | copy-start | bytes 196612
  7.2 308.0 %copy-start.1 = (bf16[1,4,4,96,256]{4,3,2,1,0:T(8,128)(2,1)S(1)}, bf16[1,4,4,96,256]{4,3,2,1,0:T(8,128)(2,1)}, u32[]{:S(2)}) copy-start(bf16[1,4,4,96,256]{4,3,2,1,0:T(8,128)(2,1)} %param.15) | copy-start | bytes 2359300
  7.2 269.1 %all-reduce.9.cloned.1.call-start = ((), (), s32[]{:S(2)}) async-start(), calls=%async_computation.4 | async-start | bytes 262144
  9.5 304.2 %reduce-scatter.11.cloned.1.call-start = ((), (), s32[]{:S(2)}) async-start(), calls=%async_computation.3 | async-start | bytes 147456
  10.6 304.5 %collective-permute-start.1 = (bf16[1,2,4,96,256]{4,3,2,1,0:T(8,128)(2,1)S(1)}, bf16[1,2,4,96,256]{4,3,2,1,0:T(8,128)(2,1)S(1)}, u32[]{:S(2)}, u32[]{:S(2)}) collective-permute-start(bf16[1,2,4,96,256]{4,3,2,1,0:T(8,128)(2,1)S(1)} %slice.213), channel_id=1, source_target_pairs={{1,0},{2,1},{3,2},{4,3},{5,4},{6,5},{7,6},{9,8},{10,9},{11,10},{12... | collective-permute-start | bytes 1179656 | tf_op jit(solution)/shard_map/ppermute | solution.py:17
  277.8 269.4 %reduce-scatter.9.cloned.1.call-start = ((), (), s32[]{:S(2)}) async-start(), calls=%async_computation.2 | async-start | bytes 147456
  329.4 14.0 %copy-start.3 = (bf16[3456,256]{1,0:T(8,128)(2,1)S(1)}, bf16[3456,256]{1,0:T(8,128)(2,1)}, u32[]{:S(2)}) copy-start(bf16[3456,256]{1,0:T(8,128)(2,1)} %param.13) | copy-start | bytes 5308420
  329.4 14.0 %copy-start.4 = (bf16[1,9,256,128]{3,2,1,0:T(8,128)(2,1)S(1)}, bf16[1,9,256,128]{3,2,1,0:T(8,128)(2,1)}, u32[]{:S(2)}) copy-start(bf16[1,9,256,128]{3,2,1,0:T(8,128)(2,1)} %copy.18) | copy-start | bytes 1769476
  354.3 10.8 %copy-start.2 = (bf16[1,4,4,96,128]{4,3,2,1,0:T(8,128)(2,1)S(1)}, bf16[1,4,4,96,128]{4,3,2,1,0:T(8,128)(2,1)}, u32[]{:S(2)}) copy-start(bf16[1,4,4,96,128]{4,3,2,1,0:T(8,128)(2,1)} %param.10) | copy-start | bytes 1179652
  354.3 10.8 %copy-start.6 = (f32[128]{0:T(128)S(1)}, f32[128]{0:T(128)}, u32[]{:S(2)}) copy-start(f32[128]{0:T(128)} %param.12) | copy-start | bytes 1540
  354.3 10.8 %copy-start.7 = (f32[128]{0:T(128)S(1)}, f32[128]{0:T(128)}, u32[]{:S(2)}) copy-start(f32[128]{0:T(128)} %param.11) | copy-start | bytes 1540
  380.6 6.5 %collective-permute-start = (bf16[1,2,4,96,128]{4,3,2,1,0:T(8,128)(2,1)}, bf16[1,2,4,96,128]{4,3,2,1,0:T(8,128)(2,1)S(1)}, u32[]{:S(2)}, u32[]{:S(2)}) collective-permute-start(bf16[1,2,4,96,128]{4,3,2,1,0:T(8,128)(2,1)} %slice.232), channel_id=1, source_target_pairs={{0,1},{1,2},{2,3},{3,4},{4,5},{5,6},{6,7},{8,9},{9,10},{10,11},{11... | collective-permute-start | bytes 589832 | tf_op jit(solution)/shard_map/ppermute | solution.py:17
  390.7 4.0 copy-start.5
  494.7 11.4 %collective-permute-start.2 = (f32[112,256]{1,0:T(8,128)S(1)}, f32[112,256]{1,0:T(8,128)S(1)}, u32[]{:S(2)}, u32[]{:S(2)}) collective-permute-start(f32[112,256]{1,0:T(8,128)S(1)} %fusion), channel_id=1, source_target_pairs={{0,8},{8,16},{16,24},{24,32},{32,40},{40,48},{48,56},{56,64},{64,7... | collective-permute-start | bytes 344072
  496.6 9.5 %collective-permute-start.3 = (f32[12,256]{1,0:T(8,128)S(1)}, f32[12,256]{1,0:T(8,128)S(1)}, u32[]{:S(2)}, u32[]{:S(2)}) collective-permute-start(f32[12,256]{1,0:T(8,128)S(1)} %slice.252), channel_id=1, source_target_pairs={{0,16},{8,24},{16,32},{24,40},{32,48},{40,56},{48,64},{56,72},{64,... | collective-permute-start | bytes 36872
Sparse Core Ops, SparseCore 0:
  11.2 265.0 all-reduce.8
  279.5 34.1 reduce-scatter.10
  507.5 39.7 reduce-scatter.8
where the time goes:
time: 560 us; the launch traced here: 555 us
  waiting for transfers between devices  311 us (56%)
  blocking collectives  126 us (22%)
  local copies, waits for them, and re-layouts  54.6 us (10%)
  matrix products  35.7 us (6%)
  between operations  15.5 us (3%)
  starting transfers between devices  8.24 us (1%)
    unnamed x8, waiting for transfers between devices  310 us
    unnamed x1, blocking collectives  95.1 us
    unnamed x59, local copies, waits for them, and re-layouts  25.8 us
    psum x1, blocking collectives, group_stats(): lax.psum((jnp.sum(widened, axis=(1, 2, 3, 5)), jnp.sum(widened * widened,...  18.2 us
    slice x1, local copies, waits for them, and re-layouts, body(): spatial[:, 2 - tap_t:2 - tap_t + frames].reshape(-1, KS * KS * out_width)  14 us
    dot_general x3, matrix products, body(): jnp.dot(block, w_back[tap_t], preferred_element_type=jnp.float32)  13.6 us
    psum x1, blocking collectives, body(): lax.psum((jnp.sum(grouped_grad, axis=(1, 2, 3, 5)), jnp.sum(grouped_grad...  12.6 us
  transfers between devices with their start and end apart: 7, of which 4 were waited for; matrix products, arithmetic and copies ran while one was open for 5% of the time, Pallas kernels for 0%

commit v1 on v0

v1 whole, which is shorter than its diff:
```python
import functools
import jax
import jax.numpy as jnp
from jax import lax
from jax.experimental import pallas as pl
from jax.experimental.pallas import tpu as pltpu
from jax.sharding import PartitionSpec as P

MESH = pl.DeviceIdType.MESH
GROUPS = 32
epsilon = 1e-06
TAPS = [(t, i) for t in range(3) for i in range(3)]
WIDTHS = (768, 768, 768, 768, 512)
STARTS = (0, 768, 1536, 2304, 3072)


def group_total(value):
    lane = lax.broadcasted_iota(jnp.int32, value.shape, 1)
    width = value.shape[1]
    value = value + jnp.where(lane % 2 == 0, pltpu.roll(value, width - 1, 1), pltpu.roll(value, 1, 1))
    return value + jnp.where(lane % 4 < 2, pltpu.roll(value, width - 2, 1), pltpu.roll(value, 2, 1))


def kernel(
    n_dp, n_ctx,
    clip, cot, gain, bias, conv_w, short_w,
    clip_out, clip_grad, conv_grad, short_grad,
    xall, cots, weight, weight_t, taps, back, cot_t,
    sums, sums_in, sums2, sums2_in,
    part, pair_in, ctx_out, ctx_in, total, slots, slots_in, out_buf, grad_buf,
    in_sem, halo_send, halo_recv, s_send, s_recv, s2_send, s2_recv,
    pair_send, pair_recv, a_send, a_recv, b_send, b_recv, out_sem,
):
    f32, bf16 = jnp.float32, jnp.bfloat16
    dp, ctx = lax.axis_index("dp"), lax.axis_index("ctx")
    half = dp % 2
    partner = dp + 1 - 2 * half
    members = 4 * n_ctx * 4 * 96 * 4

    loads = [
        pltpu.make_async_copy(clip, xall.at[2:6], in_sem.at[0]),
        pltpu.make_async_copy(cot, cots.at[0:4, 96:480], in_sem.at[1]),
        pltpu.make_async_copy(conv_w, weight.at[0:3456], in_sem.at[2]),
        pltpu.make_async_copy(short_w, weight.at[3456:3584], in_sem.at[3]),
    ]
    for copy in loads:
        copy.start()

    barrier = pltpu.get_barrier_semaphore()

    def greet_ctx(step, carry):
        pl.semaphore_signal(barrier, inc=1, device_id={"dp": dp, "ctx": (ctx + step) % n_ctx}, device_id_type=MESH)
        return carry

    def greet_dp(step, carry):
        pl.semaphore_signal(barrier, inc=1, device_id={"dp": (dp + step) % n_dp, "ctx": ctx}, device_id_type=MESH)
        return carry

    lax.fori_loop(1, n_ctx, greet_ctx, 0)
    lax.fori_loop(1, n_dp, greet_dp, 0)

    loads[0].wait()
    first = jnp.zeros((8, 128), f32)
    second = jnp.zeros((8, 128), f32)
    for f in range(4):
        value = xall[2 + f].astype(f32).reshape(48, 8, 128)
        first = first + jnp.sum(value, axis=0)
        second = second + jnp.sum(value * value, axis=0)
    sums[0] = first
    sums[1] = second
    sums_in[ctx] = sums[...]

    pl.semaphore_wait(barrier, n_ctx - 1 + n_dp - 1)

    def sums_copy(source, target, send, recv, peer):
        return pltpu.make_async_remote_copy(
            src_ref=source, dst_ref=target.at[ctx], send_sem=send.at[peer], recv_sem=recv.at[ctx],
            device_id={"dp": dp, "ctx": peer}, device_id_type=MESH,
        )

    def sums_arrival(source, target, send, recv, peer):
        return pltpu.make_async_remote_copy(
            src_ref=source, dst_ref=target.at[peer], send_sem=send.at[peer], recv_sem=recv.at[peer],
            device_id={"dp": dp, "ctx": peer}, device_id_type=MESH,
        )

    def each_ctx(body):
        def step(k, carry):
            body((ctx + k) % n_ctx)
            return carry
        lax.fori_loop(1, n_ctx, step, 0)

    each_ctx(lambda peer: sums_copy(sums, sums_in, s_send, s_recv, peer).start())

    after = jnp.minimum(ctx + 1, n_ctx - 1)
    before = jnp.maximum(ctx - 1, 0)
    clip_halo = pltpu.make_async_remote_copy(
        src_ref=clip.at[2:4], dst_ref=xall.at[0:2], send_sem=halo_send.at[0], recv_sem=halo_recv.at[0],
        device_id={"dp": dp, "ctx": after}, device_id_type=MESH,
    )
    cot_halo = pltpu.make_async_remote_copy(
        src_ref=cot.at[0:2], dst_ref=cots.at[4:6, 96:480], send_sem=halo_send.at[1], recv_sem=halo_recv.at[1],
        device_id={"dp": dp, "ctx": before}, device_id_type=MESH,
    )

    @pl.when(ctx < n_ctx - 1)
    def _():
        clip_halo.start()

    @pl.when(ctx > 0)
    def _():
        cot_halo.start()

    cots[:, 0:96] = jnp.zeros((6, 96, 256), bf16)
    cots[:, 480:576] = jnp.zeros((6, 96, 256), bf16)
    taps[:, 0:96] = jnp.zeros((6, 96, 384), bf16)
    taps[:, 480:576] = jnp.zeros((6, 96, 384), bf16)

    @pl.when(ctx == 0)
    def _():
        xall[0] = xall[2]
        xall[1] = xall[2]

    @pl.when(ctx == n_ctx - 1)
    def _():
        cots[4:6, 96:480] = jnp.zeros((2, 384, 256), bf16)

    column = lax.broadcasted_iota(jnp.int32, (384, 128), 0) % 96
    at_left, at_right = column == 0, column == 95

    def from_left(value):
        return jnp.where(at_left, 0.0, pltpu.roll(value, 1, 0))

    def from_right(value):
        return jnp.where(at_right, 0.0, pltpu.roll(value, 383, 0))

    loads[1].wait()
    for f in range(4):
        cot_t[:, f * 384:f * 384 + 384] = cots[f, 96:480].T
    loads[2].wait()
    loads[3].wait()
    for k in range(9):
        weight_t[k * 256:k * 256 + 256] = weight[k * 384:k * 384 + 384].T

    def joined(product):
        return from_right(product[:, 0:128]) + product[:, 128:256] + from_left(product[:, 256:384])

    def back_frame(f, carry):
        rows = jnp.concatenate([cots[f + 2 - t, (2 - i) * 96:(2 - i) * 96 + 384] for t, i in TAPS], axis=1)
        back[f] = joined(jnp.dot(rows, weight_t[...], preferred_element_type=f32))
        return carry

    lax.fori_loop(0, 2, back_frame, 0)

    @pl.when(ctx == 0)
    def _():
        lead = jnp.concatenate([cots[0, (2 - i) * 96:(2 - i) * 96 + 384] for i in range(3)] * 2, axis=1)
        second_rows = jnp.concatenate([cots[1, (2 - i) * 96:(2 - i) * 96 + 384] for i in range(3)], axis=1)
        extra = jnp.dot(lead, weight_t[0:1536], preferred_element_type=f32)
        extra = extra + jnp.dot(second_rows, weight_t[0:768], preferred_element_type=f32)
        back[0] = back[0] + joined(extra)

    each_ctx(lambda peer: sums_arrival(sums, sums_in, s_send, s_recv, peer).wait_recv())
    all_sums = jnp.sum(sums_in[...], axis=(0, 2))
    all_sums = group_total(jnp.concatenate([all_sums, jnp.zeros((6, 128), f32)], axis=0))
    mean = all_sums[0:1] / members
    variance = all_sums[1:2] / members - mean * mean
    inv = lax.rsqrt(variance + epsilon)
    gain_row, bias_row = gain[...], bias[...]

    def standard_of(f):
        return (xall[f].astype(f32) - mean) * inv

    @pl.when(ctx > 0)
    def _():
        clip_halo.wait_recv()

    def hidden_frame(f, carry):
        affine = standard_of(f) * gain_row + bias_row
        hidden = affine * jax.nn.sigmoid(affine)
        taps[f, 96:480, 0:128] = from_left(hidden).astype(bf16)
        taps[f, 96:480, 128:256] = hidden.astype(bf16)
        taps[f, 96:480, 256:384] = from_right(hidden).astype(bf16)
        return carry

    lax.fori_loop(0, 6, hidden_frame, 0)

    def pair_copy(chunk):
        lanes = pl.ds(0, WIDTHS[chunk])
        return pltpu.make_async_remote_copy(
            src_ref=part.at[chunk, :, 1 - half, :, lanes], dst_ref=pair_in.at[chunk, :, :, lanes],
            send_sem=pair_send.at[chunk], recv_sem=pair_recv.at[chunk],
            device_id={"dp": partner, "ctx": ctx}, device_id_type=MESH,
        )

    def ctx_copy(chunk, peer):
        lanes = pl.ds(0, WIDTHS[chunk])
        return pltpu.make_async_remote_copy(
            src_ref=ctx_out.at[chunk, peer, :, lanes], dst_ref=ctx_in.at[chunk, ctx, :, lanes],
            send_sem=a_send.at[chunk, peer], recv_sem=a_recv.at[chunk, ctx],
            device_id={"dp": dp, "ctx": peer}, device_id_type=MESH,
        )

    def ctx_arrival(chunk, peer):
        lanes = pl.ds(0, WIDTHS[chunk])
        return pltpu.make_async_remote_copy(
            src_ref=ctx_out.at[chunk, peer, :, lanes], dst_ref=ctx_in.at[chunk, peer, :, lanes],
            send_sem=a_send.at[chunk, peer], recv_sem=a_recv.at[chunk, peer],
            device_id={"dp": dp, "ctx": peer}, device_id_type=MESH,
        )

    def send_on(chunk):
        width = WIDTHS[chunk]
        pair_copy(chunk).wait_recv()
        ctx_out[chunk, :, :, 0:width] = (
            part[chunk, :, half, :, 0:width] + pair_in[chunk, :, :, 0:width]
        ).astype(bf16)
        each_ctx(lambda peer: ctx_copy(chunk, peer).start())

    for chunk in range(5):
        columns = [
            jnp.concatenate([taps[f + t, i * 96:i * 96 + 384] for f in range(4)], axis=0)
            for t, i in TAPS[2 * chunk:2 * chunk + 2]
        ]
        if chunk == 4:
            columns.append(jnp.concatenate([xall[2 + f] for f in range(4)], axis=0))
        product = jnp.dot(cot_t[...], jnp.concatenate(columns, axis=1), preferred_element_type=f32)
        part[chunk, :, :, :, 0:WIDTHS[chunk]] = product.reshape(n_ctx, 2, 16, WIDTHS[chunk])
        pair_copy(chunk).start()
        if chunk > 0:
            send_on(chunk - 1)

    @pl.when(ctx < n_ctx - 1)
    def _():
        cot_halo.wait_recv()

    back_frame(2, 0)
    send_on(4)
    back_frame(3, 0)

    def norm_frame(f, carry):
        standard = standard_of(f + 2)
        affine = standard * gain_row + bias_row
        logistic = jax.nn.sigmoid(affine)
        grad = back[f] * logistic * (1.0 + affine * (1.0 - logistic)) * gain_row
        back[f] = grad
        return (
            carry[0] + jnp.sum(grad.reshape(48, 8, 128), axis=0),
            carry[1] + jnp.sum((grad * standard).reshape(48, 8, 128), axis=0),
        )

    zero = jnp.zeros((8, 128), f32)
    grad_sum, cross_sum = lax.fori_loop(0, 4, norm_frame, (zero, zero))
    sums2[0] = grad_sum
    sums2[1] = cross_sum
    sums2_in[ctx] = sums2[...]
    each_ctx(lambda peer: sums_copy(sums2, sums2_in, s2_send, s2_recv, peer).start())

    def out_copy(f):
        return pltpu.make_async_copy(out_buf.at[f], clip_out.at[f], out_sem.at[f])

    def grad_copy(f):
        return pltpu.make_async_copy(grad_buf.at[f], clip_grad.at[f], out_sem.at[4 + f])

    def out_frame(f, carry):
        rows = jnp.concatenate([taps[f + t, i * 96:i * 96 + 384] for t, i in TAPS] + [xall[f + 2]], axis=1)
        out_buf[f] = jnp.dot(rows, weight[...], preferred_element_type=f32).astype(bf16)
        out_copy(f).start()
        return carry

    lax.fori_loop(0, 4, out_frame, 0)

    each_ctx(lambda peer: sums_arrival(sums2, sums2_in, s2_send, s2_recv, peer).wait_recv())
    all_sums = jnp.sum(sums2_in[...], axis=(0, 2))
    all_sums = group_total(jnp.concatenate([all_sums, jnp.zeros((6, 128), f32)], axis=0)) / members
    mean_grad, mean_cross = all_sums[0:1], all_sums[1:2]

    def grad_frame(f, carry):
        shortcut = lax.dot_general(
            cots[f, 96:480], weight[3456:3584], (((1,), (1,)), ((), ())), preferred_element_type=f32
        )
        value = (back[f] - mean_grad - standard_of(f + 2) * mean_cross) * inv + shortcut
        grad_buf[f] = value.astype(bf16)
        grad_copy(f).start()
        return carry

    lax.fori_loop(0, 4, grad_frame, 0)

    for chunk in range(5):
        width = WIDTHS[chunk]
        each_ctx(lambda peer: ctx_arrival(chunk, peer).wait_recv())
        start = part[chunk, ctx, half, :, 0:width] + pair_in[chunk, ctx, :, 0:width]
        ctx_in[chunk, ctx, :, 0:width] = jnp.zeros((16, width), bf16)
        value = start
        for source in range(n_ctx):
            value = value + ctx_in[chunk, source, :, 0:width].astype(f32)
        total[:, STARTS[chunk]:STARTS[chunk] + width] = value

    lane = lax.broadcasted_iota(jnp.int32, (16, 128), 1)
    short_lanes = total[:, 3456:3584]
    for owner in range(n_dp):
        base = 108 * owner // 128 * 128
        shift = 108 * owner - base
        piece = total[:, base:base + 256]
        if shift:
            piece = pltpu.roll(piece, 256 - shift, 1)
        tail = pltpu.roll(short_lanes, (108 - 4 * owner) % 128, 1) if (108 - 4 * owner) % 128 else short_lanes
        slots[owner] = jnp.where(lane < 108, piece[:, 0:128], tail)
    slots_in[dp] = slots[dp]

    def slot_copy(peer):
        return pltpu.make_async_remote_copy(
            src_ref=slots.at[peer], dst_ref=slots_in.at[dp], send_sem=b_send.at[peer], recv_sem=b_recv.at[dp],
            device_id={"dp": peer, "ctx": ctx}, device_id_type=MESH,
        )

    def slot_arrival(peer):
        return pltpu.make_async_remote_copy(
            src_ref=slots.at[peer], dst_ref=slots_in.at[peer], send_sem=b_send.at[peer], recv_sem=b_recv.at[peer],
            device_id={"dp": peer, "ctx": ctx}, device_id_type=MESH,
        )

    def each_dp(body):
        def step(k, carry):
            body((dp + k) % n_dp)
            return carry
        lax.fori_loop(1, n_dp, step, 0)

    each_dp(lambda peer: slot_copy(peer).start())

    each_ctx(lambda peer: sums_copy(sums, sums_in, s_send, s_recv, peer).wait_send())
    each_ctx(lambda peer: sums_copy(sums2, sums2_in, s2_send, s2_recv, peer).wait_send())

    @pl.when(ctx < n_ctx - 1)
    def _():
        clip_halo.wait_send()

    @pl.when(ctx > 0)
    def _():
        cot_halo.wait_send()

    for chunk in range(5):
        pair_copy(chunk).wait_send()
        each_ctx(lambda peer: ctx_copy(chunk, peer).wait_send())
    for f in range(4):
        out_copy(f).wait()
        grad_copy(f).wait()

    each_dp(lambda peer: slot_arrival(peer).wait_recv())
    halves = []
    for h in range(2):
        value = slots_in[h]
        for source in range(1, n_dp // 2):
            value = value + slots_in[2 * source + h]
        halves.append(value)
    turned = jnp.concatenate(halves, axis=0).T * (1.0 / (4 * n_ctx * n_dp))
    conv_grad[...] = turned[0:108]
    short_grad[...] = turned[108:112]
    each_dp(lambda peer: slot_copy(peer).wait_send())


def body(n_dp, n_ctx, clip_in, norm_gain, norm_bias, conv_weight, short_weight, out_cotangent):
    f32, bf16 = jnp.float32, jnp.bfloat16
    hbm = pl.BlockSpec(memory_space=pl.ANY)
    vmem = pl.BlockSpec(memory_space=pltpu.VMEM)
    dma = pltpu.SemaphoreType.DMA
    out, grad, conv, short = pl.pallas_call(
        functools.partial(kernel, n_dp, n_ctx),
        out_shape=(
            jax.ShapeDtypeStruct((4, 384, 256), bf16),
            jax.ShapeDtypeStruct((4, 384, 128), bf16),
            jax.ShapeDtypeStruct((108, 32), f32),
            jax.ShapeDtypeStruct((4, 32), f32),
        ),
        in_specs=[hbm, hbm, vmem, vmem, hbm, hbm],
        out_specs=(hbm, hbm, vmem, vmem),
        scratch_shapes=[
            pltpu.VMEM((6, 384, 128), bf16),
            pltpu.VMEM((6, 576, 256), bf16),
            pltpu.VMEM((3584, 256), bf16),
            pltpu.VMEM((2304, 384), bf16),
            pltpu.VMEM((6, 576, 384), bf16),
            pltpu.VMEM((4, 384, 128), f32),
            pltpu.VMEM((256, 1536), bf16),
            pltpu.VMEM((2, 8, 128), f32),
            pltpu.VMEM((n_ctx, 2, 8, 128), f32),
            pltpu.VMEM((2, 8, 128), f32),
            pltpu.VMEM((n_ctx, 2, 8, 128), f32),
            pltpu.VMEM((5, n_ctx, 2, 16, 768), f32),
            pltpu.VMEM((5, n_ctx, 16, 768), f32),
            pltpu.VMEM((5, n_ctx, 16, 768), bf16),
            pltpu.VMEM((5, n_ctx, 16, 768), bf16),
            pltpu.VMEM((16, 3584), f32),
            pltpu.VMEM((n_dp, 16, 128), f32),
            pltpu.VMEM((n_dp, 16, 128), f32),
            pltpu.VMEM((4, 384, 256), bf16),
            pltpu.VMEM((4, 384, 128), bf16),
            dma((4,)), dma((2,)), dma((2,)),
            dma((n_ctx,)), dma((n_ctx,)), dma((n_ctx,)), dma((n_ctx,)),
            dma((5,)), dma((5,)), dma((5, n_ctx)), dma((5, n_ctx)),
            dma((n_dp,)), dma((n_dp,)), dma((8,)),
        ],
        compiler_params=pltpu.CompilerParams(
            collective_id=0, has_side_effects=True, vmem_limit_bytes=52 << 20
        ),
        name="conv_block",
    )(
        clip_in.reshape(4, 384, 128), out_cotangent.reshape(4, 384, 256),
        norm_gain.reshape(1, 128), norm_bias.reshape(1, 128), conv_weight, short_weight,
    )
    return out.reshape(1, 4, 4, 96, 256), grad.reshape(1, 4, 4, 96, 128), conv, short


def solution(mesh):
    return jax.shard_map(
        functools.partial(body, mesh.shape["dp"], mesh.shape["ctx"]),
        mesh=mesh,
        in_specs=(
            P("dp", "ctx", None, None, None),
            P(),
            P(),
            P(),
            P(),
            P("dp", "ctx", None, None, None),
        ),
        out_specs=(
            P("dp", "ctx", None, None, None),
            P("dp", "ctx", None, None, None),
            P("dp", "ctx"),
            P("dp", "ctx"),
        ),
        check_vma=False,
    )
```

time: 560 us -> 57.8 us (0.10)
  waiting for transfers between devices: 311 us -> 0 us
  blocking collectives: 126 us -> 0 us
  Pallas kernels: 0 us -> 51 us
  local copies, waits for them, and re-layouts: 54.6 us -> 6.02 us
  matrix products: 35.7 us -> 0 us
  between operations: 15.5 us -> 0.65 us
  starting transfers between devices: 8.24 us -> 0 us
    unnamed x8 -> x0, waiting for transfers between devices: 310 us -> none
    unnamed x1 -> x0, blocking collectives: 95.1 us -> none
    pallas_call x0 -> x1, Pallas kernels: none -> 51 us  [body(): pl.pallas_call(functools.partial(kernel, n_dp, n_ctx), out_shape=(jax.Sha...]
    dot_general x11 -> x0, matrix products: 35.7 us -> none  [the longest x3 13.6 us: body(): jnp.dot(block, w_back[tap_t], preferred_element_type=jnp.float32)]
    psum x2 -> x0, blocking collectives: 30.7 us -> none  [the longest x1 18.2 us: group_stats(): lax.psum((jnp.sum(widened, axis=(1, 2, 3, 5)), jnp.sum(widened * widened,...]
    slice x10 -> x0, local copies, waits for them, and re-layouts: 24 us -> none  [the longest x1 14 us: body(): spatial[:, 2 - tap_t:2 - tap_t + frames].reshape(-1, KS * KS * out_width)]
    unnamed x59 -> x12, local copies, waits for them, and re-layouts: 25.8 us -> 6.02 us
  transfers between devices with their start and end apart: 7 -> 0, of which waited for: 4 -> 0; matrix products, arithmetic and copies ran while one was open for 5% -> 0% of each run, Pallas kernels for 0% -> 0%
where the time goes in v1:
time: 57.8 us; the launch traced here: 57.6 us
  Pallas kernels  51 us (88%)
  local copies, waits for them, and re-layouts  6.02 us (10%)
  between operations  0.65 us (1%)
    pallas_call x1, Pallas kernels, body(): pl.pallas_call(functools.partial(kernel, n_dp, n_ctx), out_shape=(jax.Sha...  51 us
    unnamed x12, local copies, waits for them, and re-layouts  6.02 us

profile of v1, /device:TPU:1, one launch (start us, length us, event | category | flops | bytes accessed | tf_op | source)
XLA Modules:
  0.0 57.6 jit_solution(462894247321598657)
XLA Ops:
  0.6 0.0 copy-start
  0.6 1.0 %copy-done = bf16[1,4,4,96,128]{4,3,2,1,0:T(8,128)(2,1)S(1)} copy-done((bf16[1,4,4,96,128]{4,3,2,1,0:T(8,128)(2,1)S(1)}, bf16[1,4,4,96,128]{4,3,2,1,0:T(8,128)(2,1)}, u32[]{:S(2)}) %copy-start) | copy-done | bytes 393240
  1.6 0.0 copy-start.1
  1.6 0.8 %copy-done.1 = bf16[128,256]{1,0:T(8,128)(2,1)S(1)} copy-done((bf16[128,256]{1,0:T(8,128)(2,1)S(1)}, bf16[128,256]{1,0:T(8,128)(2,1)}, u32[]{:S(2)}) %copy-start.1) | copy-done | bytes 65560
  2.5 0.0 copy-start.2
  2.5 0.7 %copy-done.2 = f32[128]{0:T(128)S(1)} copy-done((f32[128]{0:T(128)S(1)}, f32[128]{0:T(128)}, u32[]{:S(2)}) %copy-start.2) | copy-done | bytes 536
  3.1 0.0 copy-start.3
  3.1 0.7 %copy-done.3 = f32[128]{0:T(128)S(1)} copy-done((f32[128]{0:T(128)S(1)}, f32[128]{0:T(128)}, u32[]{:S(2)}) %copy-start.3) | copy-done | bytes 536
  3.8 51.0 %conv_block.1 = (bf16[4,384,256]{2,1,0:T(8,128)(2,1)S(1)}, bf16[4,384,128]{2,1,0:T(8,128)(2,1)S(1)}, f32[108,32]{1,0:T(8,128)S(1)}, f32[4,32]{1,0:T(4,128)S(1)}) custom-call(bf16[4,384,128]{2,1,0:T(8,128)(2,1)S(1)} %bitcast.8, bf16[4,384,256]{2,1,0:T(8,128)(2,1)} %bitcast.11, f32[1,128]{1,0:T(1,128)S(1)} %bitcast.9, f32[1,128]{1,0:T(1,128)S(1)} %bitcast.10, ...), custom_call_target="tpu_custom_call" | custom-call | tf_op jit(solution)/shard_map/conv_block/pallas_call | solution.py:367
  54.8 0.7 %copy.10 = f32[108,32]{0,1:T(8,128)} copy(f32[108,32]{1,0:T(8,128)S(1)} %get-tuple-element.14) | data formatting | bytes 27648
  55.4 0.9 %copy.14 = bf16[1,4,4,96,256]{4,3,2,1,0:T(8,128)(2,1)} copy(bf16[1,4,4,96,256]{4,3,2,1,0:T(8,128)(2,1)S(1)} %bitcast.6) | data formatting | bytes 1572864
  56.3 0.7 %copy.15 = bf16[1,4,4,96,128]{4,3,2,1,0:T(8,128)(2,1)} copy(bf16[1,4,4,96,128]{4,3,2,1,0:T(8,128)(2,1)S(1)} %bitcast.7) | data formatting | bytes 786432
  57.1 0.6 %copy.16 = f32[4,32]{1,0:T(4,128)} copy(f32[4,32]{1,0:T(4,128)S(1)} %get-tuple-element.23) | data formatting | bytes 1024
Async XLA Ops:
  0.6 1.0 %copy-start = (bf16[1,4,4,96,128]{4,3,2,1,0:T(8,128)(2,1)S(1)}, bf16[1,4,4,96,128]{4,3,2,1,0:T(8,128)(2,1)}, u32[]{:S(2)}) copy-start(bf16[1,4,4,96,128]{4,3,2,1,0:T(8,128)(2,1)} %param.6) | copy-start | bytes 1179652
  1.6 0.8 %copy-start.1 = (bf16[128,256]{1,0:T(8,128)(2,1)S(1)}, bf16[128,256]{1,0:T(8,128)(2,1)}, u32[]{:S(2)}) copy-start(bf16[128,256]{1,0:T(8,128)(2,1)} %short_w.1) | copy-start | bytes 196612
  2.5 0.7 %copy-start.2 = (f32[128]{0:T(128)S(1)}, f32[128]{0:T(128)}, u32[]{:S(2)}) copy-start(f32[128]{0:T(128)} %param.7) | copy-start | bytes 1540
  3.1 0.7 %copy-start.3 = (f32[128]{0:T(128)S(1)}, f32[128]{0:T(128)}, u32[]{:S(2)}) copy-start(f32[128]{0:T(128)} %param.8) | copy-start | bytes 1540

commit v2 on v1

v2 whole, which is shorter than its diff:
```python
import functools
import jax
import jax.numpy as jnp
from jax import lax
from jax.experimental import pallas as pl
from jax.experimental.pallas import tpu as pltpu
from jax.sharding import PartitionSpec as P

MESH = pl.DeviceIdType.MESH
GROUPS = 32
epsilon = 1e-06
TAPS = [(t, i) for t in range(3) for i in range(3)]
CHUNKS = ((2304, 1280), (1152, 1152), (0, 1152))
Y_FIRST = (3, 1)
X_FIRST = (2, 0)


def group_total(value):
    lane = lax.broadcasted_iota(jnp.int32, value.shape, 1)
    width = value.shape[1]
    value = value + jnp.where(lane % 2 == 0, pltpu.roll(value, width - 1, 1), pltpu.roll(value, 1, 1))
    return value + jnp.where(lane % 4 < 2, pltpu.roll(value, width - 2, 1), pltpu.roll(value, 2, 1))


def kernel(
    n_dp, n_ctx,
    clip, cot, gain, bias, conv_w, short_w,
    clip_out, clip_grad, conv_grad, short_grad,
    xall, cots, gain_buf, bias_buf, weight, weight_t, taps, back, edge, edge_in, cot_t,
    sums, sums_in, sums2, sums2_in,
    part, pair_in, total, y_out, y_in, x_out, x_in, step2, step2_in, step3, step3_in,
    out_buf, grad_buf, conv_buf, short_buf,
    in_sem, halo_send, halo_recv, s_send, s_recv, s2_send, s2_recv,
    pair_send, pair_recv, r1_send, r1_recv, r2_send, r2_recv, r3_send, r3_recv, out_sem,
):
    f32, bf16 = jnp.float32, jnp.bfloat16
    dp, ctx = lax.axis_index("dp"), lax.axis_index("ctx")
    z_hi, x, core = dp // 8, dp // 2 % 4, dp % 2
    y, z_lo = ctx // 2, ctx % 2
    members = 4 * n_ctx * 4 * 96 * 4

    def dp_of(z_hi, x, core):
        return (z_hi * 4 + x) * 2 + core

    def ctx_of(y, z_lo):
        return y * 2 + z_lo

    loads = [
        pltpu.make_async_copy(clip, xall.at[2:6], in_sem.at[0]),
        pltpu.make_async_copy(cot, cots.at[:, 96:480], in_sem.at[1]),
        pltpu.make_async_copy(conv_w, weight.at[0:3456], in_sem.at[2]),
        pltpu.make_async_copy(short_w, weight.at[3456:3584], in_sem.at[3]),
        pltpu.make_async_copy(gain, gain_buf, in_sem.at[4]),
        pltpu.make_async_copy(bias, bias_buf, in_sem.at[5]),
    ]
    for copy in loads:
        copy.start()

    barrier = pltpu.get_barrier_semaphore()

    def greet(peer_dp, peer_ctx):
        pl.semaphore_signal(barrier, inc=1, device_id={"dp": peer_dp, "ctx": peer_ctx}, device_id_type=MESH)

    greetings = 0
    for dz in range(4):
        for dl in range(2):
            for dc in range(2):
                if dz or dc:
                    greet(dp_of((z_hi + 4 - dz) % 4, x, (core + dc) % 2), ctx_of(y, (z_lo + dl) % 2))
                    greetings += 1
    for k in range(1, 4):
        greet(dp_of(z_hi, (x + k) % 4, core), ctx)
        greetings += 1
    for k in range(1, n_ctx):
        greet(dp, (ctx + k) % n_ctx)
        greetings += 1

    loads[0].wait()
    first = jnp.zeros((8, 128), f32)
    second = jnp.zeros((8, 128), f32)
    for f in range(4):
        value = xall[2 + f].astype(f32).reshape(48, 8, 128)
        first = first + jnp.sum(value, axis=0)
        second = second + jnp.sum(value * value, axis=0)
    sums[0] = first
    sums[1] = second
    sums_in[ctx] = sums[...]

    pl.semaphore_wait(barrier, greetings)

    def sums_copy(source, target, send, recv, peer):
        return pltpu.make_async_remote_copy(
            src_ref=source, dst_ref=target.at[ctx], send_sem=send.at[peer], recv_sem=recv.at[ctx],
            device_id={"dp": dp, "ctx": peer}, device_id_type=MESH,
        )

    def sums_arrival(source, target, send, recv, peer):
        return pltpu.make_async_remote_copy(
            src_ref=source, dst_ref=target.at[peer], send_sem=send.at[peer], recv_sem=recv.at[peer],
            device_id={"dp": dp, "ctx": peer}, device_id_type=MESH,
        )

    def each_ctx(body):
        for k in range(1, n_ctx):
            body((ctx + k) % n_ctx)

    each_ctx(lambda peer: sums_copy(sums, sums_in, s_send, s_recv, peer).start())

    clip_halo = pltpu.make_async_remote_copy(
        src_ref=xall.at[4:6], dst_ref=xall.at[0:2], send_sem=halo_send.at[0], recv_sem=halo_recv.at[0],
        device_id={"dp": dp, "ctx": jnp.minimum(ctx + 1, n_ctx - 1)}, device_id_type=MESH,
    )
    edge_halo = pltpu.make_async_remote_copy(
        src_ref=edge, dst_ref=edge_in, send_sem=halo_send.at[1], recv_sem=halo_recv.at[1],
        device_id={"dp": dp, "ctx": jnp.maximum(ctx - 1, 0)}, device_id_type=MESH,
    )

    @pl.when(ctx < n_ctx - 1)
    def _():
        clip_halo.start()

    cots[:, 0:96] = jnp.zeros((4, 96, 256), bf16)
    cots[:, 480:576] = jnp.zeros((4, 96, 256), bf16)
    taps[:, 0:96] = jnp.zeros((6, 96, 384), bf16)
    taps[:, 480:576] = jnp.zeros((6, 96, 384), bf16)

    @pl.when(ctx == 0)
    def _():
        xall[0] = xall[2]
        xall[1] = xall[2]

    column = lax.broadcasted_iota(jnp.int32, (384, 128), 0) % 96
    at_left, at_right = column == 0, column == 95

    def from_left(value):
        return jnp.where(at_left, 0.0, pltpu.roll(value, 1, 0))

    def from_right(value):
        return jnp.where(at_right, 0.0, pltpu.roll(value, 383, 0))

    loads[1].wait()
    for f in range(4):
        cot_t[:, f * 384:f * 384 + 384] = cots[f, 96:480].T
    for copy in loads[2:]:
        copy.wait()
    for k in range(9):
        weight_t[k * 256:k * 256 + 256] = weight[k * 384:k * 384 + 384].T

    def back_terms(f, frame_taps):
        rows = jnp.concatenate(
            [cots[f + 2 - t, (2 - i) * 96:(2 - i) * 96 + 384] for t in frame_taps for i in range(3)], axis=1
        )
        turned = weight_t[frame_taps[0] * 768:frame_taps[-1] * 768 + 768]
        product = jnp.dot(rows, turned, preferred_element_type=f32)
        return from_right(product[:, 0:128]) + product[:, 128:256] + from_left(product[:, 256:384])

    ahead = back_terms(-2, (0,)), back_terms(-1, (0, 1))
    back[0] = back_terms(0, (0, 1, 2))

    @pl.when(ctx == 0)
    def _():
        back[0] = back[0] + (ahead[0] + ahead[1])

    edge[0] = ahead[0].astype(bf16)
    edge[1] = ahead[1].astype(bf16)

    @pl.when(ctx > 0)
    def _():
        edge_halo.start()

    back[1] = back_terms(1, (0, 1, 2))

    each_ctx(lambda peer: sums_arrival(sums, sums_in, s_send, s_recv, peer).wait_recv())
    all_sums = jnp.sum(sums_in[...], axis=(0, 2))
    all_sums = group_total(jnp.concatenate([all_sums, jnp.zeros((6, 128), f32)], axis=0))
    mean = all_sums[0:1] / members
    variance = all_sums[1:2] / members - mean * mean
    inv = lax.rsqrt(variance + epsilon)
    gain_row, bias_row = gain_buf[...], bias_buf[...]

    def standard_of(f):
        return (xall[f].astype(f32) - mean) * inv

    def hidden_frame(f, carry):
        affine = standard_of(f) * gain_row + bias_row
        hidden = affine * jax.nn.sigmoid(affine)
        taps[f, 96:480, 0:128] = from_left(hidden).astype(bf16)
        taps[f, 96:480, 128:256] = hidden.astype(bf16)
        taps[f, 96:480, 256:384] = from_right(hidden).astype(bf16)
        return carry

    lax.fori_loop(2, 6, hidden_frame, 0)

    def pair_copy(chunk):
        lanes = pl.ds(0, CHUNKS[chunk][1])
        return pltpu.make_async_remote_copy(
            src_ref=part.at[chunk, :, 1 - core, :, lanes], dst_ref=pair_in.at[chunk, :, :, lanes],
            send_sem=pair_send.at[chunk], recv_sem=pair_recv.at[chunk],
            device_id={"dp": dp + 1 - 2 * core, "ctx": ctx}, device_id_type=MESH,
        )

    def multiply(chunk):
        t = 2 - chunk
        columns = [
            jnp.concatenate([taps[f + t, i * 96:i * 96 + 384] for f in range(4)], axis=0) for i in range(3)
        ]
        if chunk == 0:
            columns.append(jnp.concatenate([xall[2 + f] for f in range(4)], axis=0))
        width = CHUNKS[chunk][1]
        product = jnp.dot(cot_t[...], jnp.concatenate(columns, axis=1), preferred_element_type=f32)
        part[chunk, :, :, :, 0:width] = product.reshape(n_ctx, 2, 16, width)
        pair_copy(chunk).start()

    def add_pair(chunk):
        start, width = CHUNKS[chunk]
        pair_copy(chunk).wait_recv()
        value = part[chunk, :, core, :, 0:width] + pair_in[chunk, :, :, 0:width]
        total[:, start:start + width] = value.reshape(n_ctx * 16, width)

    def peer_at(along_y, k):
        if along_y:
            place = (y + k) % 4
            return place, {"dp": dp, "ctx": ctx_of(place, z_lo)}
        place = (x + k) % 4
        return place, {"dp": dp_of(z_hi, place, core), "ctx": ctx}

    def first_step(quarter, k, arriving=False):
        along_y = quarter in Y_FIRST
        source, target = (y_out, y_in) if along_y else (x_out, x_in)
        row = (Y_FIRST if along_y else X_FIRST).index(quarter)
        place, device = peer_at(along_y, k)
        slot = place if arriving else (y if along_y else x)
        return pltpu.make_async_remote_copy(
            src_ref=source.at[row, place], dst_ref=target.at[row, slot],
            send_sem=r1_send.at[quarter, place], recv_sem=r1_recv.at[quarter, slot],
            device_id=device, device_id_type=MESH,
        )

    def second_step(quarter, k, arriving=False):
        along_y = quarter in X_FIRST
        place, device = peer_at(along_y, k)
        slot = place if arriving else (y if along_y else x)
        return pltpu.make_async_remote_copy(
            src_ref=step2.at[quarter, place], dst_ref=step2_in.at[quarter, slot],
            send_sem=r2_send.at[quarter, place], recv_sem=r2_recv.at[quarter, slot],
            device_id=device, device_id_type=MESH,
        )

    def third_step(quarter, to_lo, to_core):
        return pltpu.make_async_remote_copy(
            src_ref=step3.at[quarter, to_lo, to_core], dst_ref=step3_in.at[z_hi * 2 + z_lo, core],
            send_sem=r3_send.at[quarter, to_lo, to_core], recv_sem=r3_recv.at[z_hi * 2 + z_lo, core],
            device_id={"dp": dp_of(quarter, x, to_core), "ctx": ctx_of(y, to_lo)}, device_id_type=MESH,
        )

    def third_arrival(from_z, from_core):
        return pltpu.make_async_remote_copy(
            src_ref=step3.at[0, 0, 0], dst_ref=step3_in.at[from_z, from_core],
            send_sem=r3_send.at[0, 0, 0], recv_sem=r3_recv.at[from_z, from_core],
            device_id={"dp": dp_of(from_z // 2, x, from_core), "ctx": ctx_of(y, from_z % 2)}, device_id_type=MESH,
        )

    lane = lax.broadcasted_iota(jnp.int32, (128, 128), 1)

    def begin(quarter):
        short_lanes = total[:, 3456:3584]
        for place in range(8):
            owner = 8 * quarter + place
            base = 108 * owner // 128 * 128
            shift = 108 * owner - base
            value = total[:, base:base + 256]
            if shift:
                value = pltpu.roll(value, 256 - shift, 1)
            tail = (108 - 4 * owner) % 128
            tail = pltpu.roll(short_lanes, tail, 1) if tail else short_lanes
            value = jnp.where(lane < 108, value[:, 0:128], tail).astype(bf16)
            if quarter in Y_FIRST:
                y_out[Y_FIRST.index(quarter), :, :, place * 128:place * 128 + 128] = value.reshape(4, 32, 128)
            else:
                at = place % 2 * 128
                x_out[X_FIRST.index(quarter), place // 2, :, at:at + 128] = value
        for k in (1, 3, 2):
            first_step(quarter, k).start()
        if quarter in Y_FIRST:
            y_in[Y_FIRST.index(quarter), y] = y_out[Y_FIRST.index(quarter), y]
        else:
            x_in[X_FIRST.index(quarter), x] = x_out[X_FIRST.index(quarter), x]

    def go_on(quarter):
        for k in (1, 3, 2):
            first_step(quarter, k, arriving=True).wait_recv()
        along_y = quarter in Y_FIRST
        arrived = y_in if along_y else x_in
        row = (Y_FIRST if along_y else X_FIRST).index(quarter)
        value = arrived[row, 0].astype(f32)
        for place in range(1, 4):
            value = value + arrived[row, place].astype(f32)
        if along_y:
            for place in range(4):
                step2[quarter, place] = value[:, place * 256:place * 256 + 256]
        else:
            step2[quarter] = value.reshape(4, 32, 256)
        for k in (1, 3, 2):
            second_step(quarter, k).start()
        own = x if along_y else y
        step2_in[quarter, own] = step2[quarter, own]

    def finish(quarter):
        for k in (1, 3, 2):
            second_step(quarter, k, arriving=True).wait_recv()
        value = step2_in[quarter, 0]
        for place in range(1, 4):
            value = value + step2_in[quarter, place]
        for to_lo in range(2):
            for to_core in range(2):
                step3[quarter, to_lo, to_core] = value[to_lo * 16:to_lo * 16 + 16, to_core * 128:to_core * 128 + 128]
                mine = (z_hi == quarter) & (z_lo == to_lo) & (core == to_core)

                @pl.when(jnp.logical_not(mine))
                def _():
                    third_step(quarter, to_lo, to_core).start()

                @pl.when(mine)
                def _():
                    step3_in[z_hi * 2 + z_lo, core] = step3[quarter, to_lo, to_core]

    multiply(0)

    @pl.when(ctx > 0)
    def _():
        clip_halo.wait_recv()

    lax.fori_loop(0, 2, hidden_frame, 0)
    multiply(1)
    add_pair(0)
    begin(3)
    multiply(2)
    add_pair(1)
    begin(2)
    back[2] = back_terms(2, (1, 2))
    add_pair(2)
    begin(1)
    begin(0)

    back[3] = back_terms(3, (2,))

    @pl.when(ctx < n_ctx - 1)
    def _():
        edge_halo.wait_recv()
        back[2] = back[2] + edge_in[0].astype(f32)
        back[3] = back[3] + edge_in[1].astype(f32)

    def norm_frame(f, carry):
        standard = standard_of(f + 2)
        affine = standard * gain_row + bias_row
        logistic = jax.nn.sigmoid(affine)
        grad = back[f] * logistic * (1.0 + affine * (1.0 - logistic)) * gain_row
        back[f] = grad
        return (
            carry[0] + jnp.sum(grad.reshape(48, 8, 128), axis=0),
            carry[1] + jnp.sum((grad * standard).reshape(48, 8, 128), axis=0),
        )

    zero = jnp.zeros((8, 128), f32)
    grad_sum, cross_sum = lax.fori_loop(0, 4, norm_frame, (zero, zero))
    sums2[0] = grad_sum
    sums2[1] = cross_sum
    sums2_in[ctx] = sums2[...]
    each_ctx(lambda peer: sums_copy(sums2, sums2_in, s2_send, s2_recv, peer).start())

    def out_copy(f):
        return pltpu.make_async_copy(out_buf.at[f], clip_out.at[f], out_sem.at[f])

    def grad_copy(f):
        return pltpu.make_async_copy(grad_buf.at[f], clip_grad.at[f], out_sem.at[4 + f])

    def out_frame(f, carry):
        rows = jnp.concatenate([taps[f + t, i * 96:i * 96 + 384] for t, i in TAPS] + [xall[f + 2]], axis=1)
        out_buf[f] = jnp.dot(rows, weight[...], preferred_element_type=f32).astype(bf16)
        out_copy(f).start()
        return carry

    go_on(3)
    go_on(2)
    lax.fori_loop(0, 1, out_frame, 0)
    go_on(1)
    go_on(0)
    lax.fori_loop(1, 3, out_frame, 0)
    for quarter in (3, 2, 1, 0):
        finish(quarter)
    lax.fori_loop(3, 4, out_frame, 0)

    each_ctx(lambda peer: sums_arrival(sums2, sums2_in, s2_send, s2_recv, peer).wait_recv())
    all_sums = jnp.sum(sums2_in[...], axis=(0, 2))
    all_sums = group_total(jnp.concatenate([all_sums, jnp.zeros((6, 128), f32)], axis=0)) / members
    mean_grad, mean_cross = all_sums[0:1], all_sums[1:2]

    def grad_frame(f, carry):
        shortcut = lax.dot_general(
            cots[f, 96:480], weight[3456:3584], (((1,), (1,)), ((), ())), preferred_element_type=f32
        )
        value = (back[f] - mean_grad - standard_of(f + 2) * mean_cross) * inv + shortcut
        grad_buf[f] = value.astype(bf16)
        grad_copy(f).start()
        return carry

    lax.fori_loop(0, 4, grad_frame, 0)

    each_ctx(lambda peer: sums_copy(sums, sums_in, s_send, s_recv, peer).wait_send())
    each_ctx(lambda peer: sums_copy(sums2, sums2_in, s2_send, s2_recv, peer).wait_send())

    @pl.when(ctx < n_ctx - 1)
    def _():
        clip_halo.wait_send()

    @pl.when(ctx > 0)
    def _():
        edge_halo.wait_send()

    for chunk in range(3):
        pair_copy(chunk).wait_send()
    for quarter in range(4):
        for k in range(1, 4):
            first_step(quarter, k).wait_send()
            second_step(quarter, k).wait_send()
    for f in range(4):
        out_copy(f).wait()
        grad_copy(f).wait()
    for quarter in range(4):
        for to_lo in range(2):
            for to_core in range(2):
                mine = (z_hi == quarter) & (z_lo == to_lo) & (core == to_core)

                @pl.when(jnp.logical_not(mine))
                def _():
                    third_step(quarter, to_lo, to_core).wait_send()

    for from_z in range(8):
        for from_core in range(2):
            mine = (z_hi * 2 + z_lo == from_z) & (core == from_core)

            @pl.when(jnp.logical_not(mine))
            def _():
                third_arrival(from_z, from_core).wait_recv()

    halves = []
    for h in range(2):
        value = step3_in[0, h]
        for from_z in range(1, 8):
            value = value + step3_in[from_z, h]
        halves.append(value)
    value = jnp.concatenate(halves, axis=0) * (1.0 / (4 * n_ctx * n_dp))
    conv_buf[...] = value[:, 0:108]
    short_buf[...] = value.T[108:112]
    ends = [
        pltpu.make_async_copy(conv_buf, conv_grad, out_sem.at[8]),
        pltpu.make_async_copy(short_buf, short_grad, out_sem.at[9]),
    ]
    for copy in ends:
        copy.start()
    for copy in ends:
        copy.wait()


def store(*refs):
    sources, targets, sems = refs[0:4], refs[4:8], refs[8]
    copies = [pltpu.make_async_copy(sources[k], targets[k], sems.at[k]) for k in range(4)]
    for copy in copies:
        copy.start()
    for copy in copies:
        copy.wait()


def body(n_dp, n_ctx, clip_in, norm_gain, norm_bias, conv_weight, short_weight, out_cotangent):
    f32, bf16 = jnp.float32, jnp.bfloat16
    anywhere = pl.BlockSpec(memory_space=pl.ANY)
    hbm = pl.BlockSpec(memory_space=pltpu.HBM)
    dma = pltpu.SemaphoreType.DMA
    shapes = (
        jax.ShapeDtypeStruct((4, 384, 256), bf16),
        jax.ShapeDtypeStruct((4, 384, 128), bf16),
        jax.ShapeDtypeStruct((32, 108), f32),
        jax.ShapeDtypeStruct((4, 32), f32),
    )
    results = pl.pallas_call(
        functools.partial(kernel, n_dp, n_ctx),
        out_shape=shapes,
        in_specs=[hbm] * 6,
        out_specs=(anywhere,) * 4,
        scratch_shapes=[
            pltpu.VMEM((6, 384, 128), bf16),
            pltpu.VMEM((4, 576, 256), bf16),
            pltpu.VMEM((1, 128), f32),
            pltpu.VMEM((1, 128), f32),
            pltpu.VMEM((3584, 256), bf16),
            pltpu.VMEM((2304, 384), bf16),
            pltpu.VMEM((6, 576, 384), bf16),
            pltpu.VMEM((4, 384, 128), f32),
            pltpu.VMEM((2, 384, 128), bf16),
            pltpu.VMEM((2, 384, 128), bf16),
            pltpu.VMEM((256, 1536), bf16),
            pltpu.VMEM((2, 8, 128), f32),
            pltpu.VMEM((n_ctx, 2, 8, 128), f32),
            pltpu.VMEM((2, 8, 128), f32),
            pltpu.VMEM((n_ctx, 2, 8, 128), f32),
            pltpu.VMEM((3, n_ctx, 2, 16, 1280), f32),
            pltpu.VMEM((3, n_ctx, 16, 1280), f32),
            pltpu.VMEM((128, 3584), f32),
            pltpu.VMEM((2, 4, 32, 1024), bf16),
            pltpu.VMEM((2, 4, 32, 1024), bf16),
            pltpu.VMEM((2, 4, 128, 256), bf16),
            pltpu.VMEM((2, 4, 128, 256), bf16),
            pltpu.VMEM((4, 4, 32, 256), f32),
            pltpu.VMEM((4, 4, 32, 256), f32),
            pltpu.VMEM((4, 2, 2, 16, 128), f32),
            pltpu.VMEM((8, 2, 16, 128), f32),
            pltpu.VMEM((4, 384, 256), bf16),
            pltpu.VMEM((4, 384, 128), bf16),
            pltpu.VMEM((32, 108), f32),
            pltpu.VMEM((4, 32), f32),
            dma((6,)), dma((2,)), dma((2,)),
            dma((n_ctx,)), dma((n_ctx,)), dma((n_ctx,)), dma((n_ctx,)),
            dma((3,)), dma((3,)), dma((4, 4)), dma((4, 4)), dma((4, 4)), dma((4, 4)),
            dma((4, 2, 2)), dma((8, 2)), dma((10,)),
        ],
        compiler_params=pltpu.CompilerParams(
            collective_id=0, has_side_effects=True, vmem_limit_bytes=48 << 20
        ),
        name="conv_block",
    )(
        *[pltpu.with_memory_space_constraint(v, pltpu.HBM) for v in (clip_in.reshape(4, 384, 128), out_cotangent.reshape(4, 384, 256),
        norm_gain.reshape(1, 128), norm_bias.reshape(1, 128), conv_weight, short_weight)]
    )
    out, grad, conv, short = pl.pallas_call(
        store,
        out_shape=shapes,
        in_specs=[anywhere] * 4,
        out_specs=(anywhere,) * 4,
        scratch_shapes=[dma((4,))],
        name="store",
    )(*[pltpu.with_memory_space_constraint(v, pltpu.VMEM) for v in results])
    return out.reshape(1, 4, 4, 96, 256), grad.reshape(1, 4, 4, 96, 128), conv.T, short


def solution(mesh):
    return jax.shard_map(
        functools.partial(body, mesh.shape["dp"], mesh.shape["ctx"]),
        mesh=mesh,
        in_specs=(
            P("dp", "ctx", None, None, None),
            P(),
            P(),
            P(),
            P(),
            P("dp", "ctx", None, None, None),
        ),
        out_specs=(
            P("dp", "ctx", None, None, None),
            P("dp", "ctx", None, None, None),
            P("dp", "ctx"),
            P("dp", "ctx"),
        ),
        check_vma=False,
    )
```

time: 57.8 us -> 43.1 us (0.75)
  Pallas kernels: 51 us -> 42.4 us
  local copies, waits for them, and re-layouts: 6.02 us -> 0 us
    pallas_call x1 -> x2, Pallas kernels: 51 us -> 42.4 us  [the longest x1 41.3 us: body(): pl.pallas_call(functools.partial(kernel, n_dp, n_ctx), out_shape=shapes,...]
    unnamed x12 -> x0, local copies, waits for them, and re-layouts: 6.02 us -> none
where the time goes in v2:
time: 43.1 us; the launch traced here: 43 us
  Pallas kernels  42.4 us (98%)
  between operations  0.64 us (1%)
    pallas_call x1, Pallas kernels, body(): pl.pallas_call(functools.partial(kernel, n_dp, n_ctx), out_shape=shapes,...  41.3 us
    pallas_call x1, Pallas kernels, body(): pl.pallas_call(store, out_shape=shapes, in_specs=[anywhere] * 4, out_spec...  1.05 us

profile of v2, /device:TPU:1, one launch (start us, length us, event | category | flops | bytes accessed | tf_op | source)
XLA Modules:
  0.0 43.0 jit_solution(2344524293938837628)
XLA Ops:
  0.6 41.3 %conv_block.1 = (bf16[4,384,256]{2,1,0:T(8,128)(2,1)S(1)}, bf16[4,384,128]{2,1,0:T(8,128)(2,1)S(1)}, f32[32,108]{1,0:T(8,128)S(1)}, f32[4,32]{1,0:T(4,128)S(1)}) custom-call(bf16[4,384,128]{2,1,0:T(8,128)(2,1)} %bitcast.8, bf16[4,384,256]{2,1,0:T(8,128)(2,1)} %bitcast.7, f32[1,128]{1,0:T(1,128)} %bitcast.9, f32[1,128]{1,0:T(1,128)} %bitcast.10, ...), custom_call_target="tpu_custom_call" | custom-call | tf_op jit(solution)/shard_map/conv_block/pallas_call | solution.py:485
  41.9 1.0 %store.1 = (bf16[4,384,256]{2,1,0:T(8,128)(2,1)}, bf16[4,384,128]{2,1,0:T(8,128)(2,1)}, f32[32,108]{1,0:T(8,128)}, f32[4,32]{1,0:T(4,128)}) custom-call(bf16[4,384,256]{2,1,0:T(8,128)(2,1)S(1)} %get-tuple-element.12.refs_0_, bf16[4,384,128]{2,1,0:T(8,128)(2,1)S(1)} %get-tuple-element.13.refs_1_, f32[32,108]{1,0:T(8,128)S(1)} %get-tuple-element.14.refs_2_, ...), custom_call_target="tpu_custom_call" | custom-call | tf_op jit(solution)/shard_map/store/pallas_call | solution.py:534

commit v3 on v2

--- a/solution.py
+++ b/solution.py
@@ -11,8 +11,7 @@
 epsilon = 1e-06
 TAPS = [(t, i) for t in range(3) for i in range(3)]
 CHUNKS = ((2304, 1280), (1152, 1152), (0, 1152))
-Y_FIRST = (3, 1)
-X_FIRST = (2, 0)
+Y_FIRST, X_FIRST = 0, 1
 
 
 def group_total(value):
@@ -224,25 +223,24 @@
         place = (x + k) % 4
         return place, {"dp": dp_of(z_hi, place, core), "ctx": ctx}
 
-    def first_step(quarter, k, arriving=False):
-        along_y = quarter in Y_FIRST
+    def first_step(quarter, kind, k, arriving=False):
+        along_y = kind == Y_FIRST
         source, target = (y_out, y_in) if along_y else (x_out, x_in)
-        row = (Y_FIRST if along_y else X_FIRST).index(quarter)
         place, device = peer_at(along_y, k)
         slot = place if arriving else (y if along_y else x)
         return pltpu.make_async_remote_copy(
-            src_ref=source.at[row, place], dst_ref=target.at[row, slot],
-            send_sem=r1_send.at[quarter, place], recv_sem=r1_recv.at[quarter, slot],
+            src_ref=source.at[quarter, place], dst_ref=target.at[quarter, slot],
+            send_sem=r1_send.at[quarter, kind, place], recv_sem=r1_recv.at[quarter, kind, slot],
             device_id=device, device_id_type=MESH,
         )
 
-    def second_step(quarter, k, arriving=False):
-        along_y = quarter in X_FIRST
+    def second_step(quarter, kind, k, arriving=False):
+        along_y = kind == X_FIRST
         place, device = peer_at(along_y, k)
         slot = place if arriving else (y if along_y else x)
         return pltpu.make_async_remote_copy(
-            src_ref=step2.at[quarter, place], dst_ref=step2_in.at[quarter, slot],
-            send_sem=r2_send.at[quarter, place], recv_sem=r2_recv.at[quarter, slot],
+            src_ref=step2.at[quarter, kind, place], dst_ref=step2_in.at[quarter, kind, slot],
+            send_sem=r2_send.at[quarter, kind, place], recv_sem=r2_recv.at[quarter, kind, slot],
             device_id=device, device_id_type=MESH,
         )
 
@@ -274,46 +272,45 @@
             tail = (108 - 4 * owner) % 128
             tail = pltpu.roll(short_lanes, tail, 1) if tail else short_lanes
             value = jnp.where(lane < 108, value[:, 0:128], tail).astype(bf16)
-            if quarter in Y_FIRST:
-                y_out[Y_FIRST.index(quarter), :, :, place * 128:place * 128 + 128] = value.reshape(4, 32, 128)
+            if place % 2 == Y_FIRST:
+                at = place // 2 * 128
+                y_out[quarter, :, :, at:at + 128] = value.reshape(4, 32, 128)
             else:
-                at = place % 2 * 128
-                x_out[X_FIRST.index(quarter), place // 2, :, at:at + 128] = value
-        for k in (1, 3, 2):
-            first_step(quarter, k).start()
-        if quarter in Y_FIRST:
-            y_in[Y_FIRST.index(quarter), y] = y_out[Y_FIRST.index(quarter), y]
-        else:
-            x_in[X_FIRST.index(quarter), x] = x_out[X_FIRST.index(quarter), x]
+                x_out[quarter, place // 2] = value
+        for k in (2, 1, 3):
+            first_step(quarter, Y_FIRST, k).start()
+            first_step(quarter, X_FIRST, k).start()
+        y_in[quarter, y] = y_out[quarter, y]
+        x_in[quarter, x] = x_out[quarter, x]
 
     def go_on(quarter):
-        for k in (1, 3, 2):
-            first_step(quarter, k, arriving=True).wait_recv()
-        along_y = quarter in Y_FIRST
-        arrived = y_in if along_y else x_in
-        row = (Y_FIRST if along_y else X_FIRST).index(quarter)
-        value = arrived[row, 0].astype(f32)
-        for place in range(1, 4):
-            value = value + arrived[row, place].astype(f32)
-        if along_y:
-            for place in range(4):
-                step2[quarter, place] = value[:, place * 256:place * 256 + 256]
-        else:
-            step2[quarter] = value.reshape(4, 32, 256)
-        for k in (1, 3, 2):
-            second_step(quarter, k).start()
-        own = x if along_y else y
-        step2_in[quarter, own] = step2[quarter, own]
+        for kind, arrived in ((Y_FIRST, y_in), (X_FIRST, x_in)):
+            for k in (1, 3, 2):
+                first_step(quarter, kind, k, arriving=True).wait_recv()
+            value = arrived[quarter, 0].astype(f32)
+            for place in range(1, 4):
+                value = value + arrived[quarter, place].astype(f32)
+            if kind == Y_FIRST:
+                for place in range(4):
+                    step2[quarter, kind, place] = value[:, place * 128:place * 128 + 128]
+            else:
+                step2[quarter, kind] = value.reshape(4, 32, 128)
+            for k in (2, 1, 3):
+                second_step(quarter, kind, k).start()
+            own = x if kind == Y_FIRST else y
+            step2_in[quarter, kind, own] = step2[quarter, kind, own]
 
     def finish(quarter):
-        for k in (1, 3, 2):
-            second_step(quarter, k, arriving=True).wait_recv()
-        value = step2_in[quarter, 0]
-        for place in range(1, 4):
-            value = value + step2_in[quarter, place]
-        for to_lo in range(2):
-            for to_core in range(2):
-                step3[quarter, to_lo, to_core] = value[to_lo * 16:to_lo * 16 + 16, to_core * 128:to_core * 128 + 128]
+        for kind in (Y_FIRST, X_FIRST):
+            to_core = kind
+            for k in (1, 3, 2):
+                second_step(quarter, kind, k, arriving=True).wait_recv()
+            value = step2_in[quarter, kind, 0]
+            for place in range(1, 4):
+                value = value + step2_in[quarter, kind, place]
+            value = value.astype(step3.dtype)
+            for to_lo in range(2):
+                step3[quarter, to_lo, to_core] = value[to_lo * 16:to_lo * 16 + 16]
                 mine = (z_hi == quarter) & (z_lo == to_lo) & (core == to_core)
 
                 @pl.when(jnp.logical_not(mine))
@@ -382,12 +379,14 @@
 
     go_on(3)
     go_on(2)
-    lax.fori_loop(0, 1, out_frame, 0)
+    lax.fori_loop(0, 2, out_frame, 0)
     go_on(1)
     go_on(0)
-    lax.fori_loop(1, 3, out_frame, 0)
-    for quarter in (3, 2, 1, 0):
-        finish(quarter)
+    finish(3)
+    finish(2)
+    lax.fori_loop(2, 3, out_frame, 0)
+    finish(1)
+    finish(0)
     lax.fori_loop(3, 4, out_frame, 0)
 
     each_ctx(lambda peer: sums_arrival(sums2, sums2_in, s2_send, s2_recv, peer).wait_recv())
@@ -420,9 +419,10 @@
     for chunk in range(3):
         pair_copy(chunk).wait_send()
     for quarter in range(4):
-        for k in range(1, 4):
-            first_step(quarter, k).wait_send()
-            second_step(quarter, k).wait_send()
+        for kind in (Y_FIRST, X_FIRST):
+            for k in range(1, 4):
+                first_step(quarter, kind, k).wait_send()
+                second_step(quarter, kind, k).wait_send()
     for f in range(4):
         out_copy(f).wait()
         grad_copy(f).wait()
@@ -445,9 +445,9 @@
 
     halves = []
     for h in range(2):
-        value = step3_in[0, h]
+        value = step3_in[0, h].astype(f32)
         for from_z in range(1, 8):
-            value = value + step3_in[from_z, h]
+            value = value + step3_in[from_z, h].astype(f32)
         halves.append(value)
     value = jnp.concatenate(halves, axis=0) * (1.0 / (4 * n_ctx * n_dp))
     conv_buf[...] = value[:, 0:108]
@@ -506,12 +506,12 @@
             pltpu.VMEM((3, n_ctx, 2, 16, 1280), f32),
             pltpu.VMEM((3, n_ctx, 16, 1280), f32),
             pltpu.VMEM((128, 3584), f32),
-            pltpu.VMEM((2, 4, 32, 1024), bf16),
-            pltpu.VMEM((2, 4, 32, 1024), bf16),
-            pltpu.VMEM((2, 4, 128, 256), bf16),
-            pltpu.VMEM((2, 4, 128, 256), bf16),
-            pltpu.VMEM((4, 4, 32, 256), f32),
-            pltpu.VMEM((4, 4, 32, 256), f32),
+            pltpu.VMEM((4, 4, 32, 512), bf16),
+            pltpu.VMEM((4, 4, 32, 512), bf16),
+            pltpu.VMEM((4, 4, 128, 128), bf16),
+            pltpu.VMEM((4, 4, 128, 128), bf16),
+            pltpu.VMEM((4, 2, 4, 32, 128), f32),
+            pltpu.VMEM((4, 2, 4, 32, 128), f32),
             pltpu.VMEM((4, 2, 2, 16, 128), f32),
             pltpu.VMEM((8, 2, 16, 128), f32),
             pltpu.VMEM((4, 384, 256), bf16),
@@ -520,7 +520,7 @@
             pltpu.VMEM((4, 32), f32),
             dma((6,)), dma((2,)), dma((2,)),
             dma((n_ctx,)), dma((n_ctx,)), dma((n_ctx,)), dma((n_ctx,)),
-            dma((3,)), dma((3,)), dma((4, 4)), dma((4, 4)), dma((4, 4)), dma((4, 4)),
+            dma((3,)), dma((3,)), dma((4, 2, 4)), dma((4, 2, 4)), dma((4, 2, 4)), dma((4, 2, 4)),
             dma((4, 2, 2)), dma((8, 2)), dma((10,)),
         ],
         compiler_params=pltpu.CompilerParams(
@@ -528,8 +528,10 @@
         ),
         name="conv_block",
     )(
-        *[pltpu.with_memory_space_constraint(v, pltpu.HBM) for v in (clip_in.reshape(4, 384, 128), out_cotangent.reshape(4, 384, 256),
-        norm_gain.reshape(1, 128), norm_bias.reshape(1, 128), conv_weight, short_weight)]
+        *[pltpu.with_memory_space_constraint(value, pltpu.HBM) for value in (
+            clip_in.reshape(4, 384, 128), out_cotangent.reshape(4, 384, 256),
+            norm_gain.reshape(1, 128), norm_bias.reshape(1, 128), conv_weight, short_weight,
+        )]
     )
     out, grad, conv, short = pl.pallas_call(
         store,
@@ -538,7 +540,7 @@
         out_specs=(anywhere,) * 4,
         scratch_shapes=[dma((4,))],
         name="store",
-    )(*[pltpu.with_memory_space_constraint(v, pltpu.VMEM) for v in results])
+    )(*[pltpu.with_memory_space_constraint(value, pltpu.VMEM) for value in results])
     return out.reshape(1, 4, 4, 96, 256), grad.reshape(1, 4, 4, 96, 128), conv.T, short
 
 

time: 43.1 us -> 41.1 us (0.954)
  Pallas kernels: 42.4 us -> 40.3 us
    pallas_call x1, Pallas kernels: 41.3 us -> 39.3 us  [body(): pl.pallas_call(functools.partial(kernel, n_dp, n_ctx), out_shape=shapes,...]
where the time goes in v3:
time: 41.1 us; the launch traced here: 41 us
  Pallas kernels  40.3 us (98%)
  between operations  0.64 us (2%)
    pallas_call x1, Pallas kernels, body(): pl.pallas_call(functools.partial(kernel, n_dp, n_ctx), out_shape=shapes,...  39.3 us
    pallas_call x1, Pallas kernels, body(): pl.pallas_call(store, out_shape=shapes, in_specs=[anywhere] * 4, out_spec...  1.05 us

profile of v3, /device:TPU:1, one launch (start us, length us, event | category | flops | bytes accessed | tf_op | source)
XLA Modules:
  0.0 41.0 jit_solution(7795730287589168106)
XLA Ops:
  0.6 39.3 %conv_block.1 = (bf16[4,384,256]{2,1,0:T(8,128)(2,1)S(1)}, bf16[4,384,128]{2,1,0:T(8,128)(2,1)S(1)}, f32[32,108]{1,0:T(8,128)S(1)}, f32[4,32]{1,0:T(4,128)S(1)}) custom-call(bf16[4,384,128]{2,1,0:T(8,128)(2,1)} %bitcast.8, bf16[4,384,256]{2,1,0:T(8,128)(2,1)} %bitcast.7, f32[1,128]{1,0:T(1,128)} %bitcast.9, f32[1,128]{1,0:T(1,128)} %bitcast.10, ...), custom_call_target="tpu_custom_call" | custom-call | tf_op jit(solution)/shard_map/conv_block/pallas_call | solution.py:485
  39.9 1.0 %store.1 = (bf16[4,384,256]{2,1,0:T(8,128)(2,1)}, bf16[4,384,128]{2,1,0:T(8,128)(2,1)}, f32[32,108]{1,0:T(8,128)}, f32[4,32]{1,0:T(4,128)}) custom-call(bf16[4,384,256]{2,1,0:T(8,128)(2,1)S(1)} %get-tuple-element.12.refs_0_, bf16[4,384,128]{2,1,0:T(8,128)(2,1)S(1)} %get-tuple-element.13.refs_1_, f32[32,108]{1,0:T(8,128)S(1)} %get-tuple-element.14.refs_2_, ...), custom_call_target="tpu_custom_call" | custom-call | tf_op jit(solution)/shard_map/store/pallas_call | solution.py:536

commit v4 on v3

--- a/solution.py
+++ b/solution.py
@@ -45,13 +45,15 @@
         return y * 2 + z_lo
 
     loads = [
-        pltpu.make_async_copy(clip, xall.at[2:6], in_sem.at[0]),
+        pltpu.make_async_copy(clip.at[0:2], xall.at[2:4], in_sem.at[0]),
         pltpu.make_async_copy(cot, cots.at[:, 96:480], in_sem.at[1]),
         pltpu.make_async_copy(conv_w, weight.at[0:3456], in_sem.at[2]),
         pltpu.make_async_copy(short_w, weight.at[3456:3584], in_sem.at[3]),
         pltpu.make_async_copy(gain, gain_buf, in_sem.at[4]),
         pltpu.make_async_copy(bias, bias_buf, in_sem.at[5]),
     ]
+    late_clip = pltpu.make_async_copy(clip.at[2:4], xall.at[4:6], in_sem.at[6])
+    late_clip.start()
     for copy in loads:
         copy.start()
 
@@ -61,6 +63,9 @@
         pl.semaphore_signal(barrier, inc=1, device_id={"dp": peer_dp, "ctx": peer_ctx}, device_id_type=MESH)
 
     greetings = 0
+    for k in range(1, n_ctx):
+        greet(dp, (ctx + k) % n_ctx)
+        greetings += 1
     for dz in range(4):
         for dl in range(2):
             for dc in range(2):
@@ -70,19 +75,18 @@
     for k in range(1, 4):
         greet(dp_of(z_hi, (x + k) % 4, core), ctx)
         greetings += 1
-    for k in range(1, n_ctx):
-        greet(dp, (ctx + k) % n_ctx)
-        greetings += 1
 
     loads[0].wait()
     first = jnp.zeros((8, 128), f32)
     second = jnp.zeros((8, 128), f32)
     for f in range(4):
+        if f == 2:
+            late_clip.wait()
         value = xall[2 + f].astype(f32).reshape(48, 8, 128)
         first = first + jnp.sum(value, axis=0)
         second = second + jnp.sum(value * value, axis=0)
-    sums[0] = first
-    sums[1] = second
+    sums[0:1] = jnp.sum(first, axis=0, keepdims=True)
+    sums[1:2] = jnp.sum(second, axis=0, keepdims=True)
     sums_in[ctx] = sums[...]
 
     pl.semaphore_wait(barrier, greetings)
@@ -170,7 +174,7 @@
     back[1] = back_terms(1, (0, 1, 2))
 
     each_ctx(lambda peer: sums_arrival(sums, sums_in, s_send, s_recv, peer).wait_recv())
-    all_sums = jnp.sum(sums_in[...], axis=(0, 2))
+    all_sums = jnp.sum(sums_in[...], axis=0)
     all_sums = group_total(jnp.concatenate([all_sums, jnp.zeros((6, 128), f32)], axis=0))
     mean = all_sums[0:1] / members
     variance = all_sums[1:2] / members - mean * mean
@@ -360,8 +364,8 @@
 
     zero = jnp.zeros((8, 128), f32)
     grad_sum, cross_sum = lax.fori_loop(0, 4, norm_frame, (zero, zero))
-    sums2[0] = grad_sum
-    sums2[1] = cross_sum
+    sums2[0:1] = jnp.sum(grad_sum, axis=0, keepdims=True)
+    sums2[1:2] = jnp.sum(cross_sum, axis=0, keepdims=True)
     sums2_in[ctx] = sums2[...]
     each_ctx(lambda peer: sums_copy(sums2, sums2_in, s2_send, s2_recv, peer).start())
 
@@ -390,7 +394,7 @@
     lax.fori_loop(3, 4, out_frame, 0)
 
     each_ctx(lambda peer: sums_arrival(sums2, sums2_in, s2_send, s2_recv, peer).wait_recv())
-    all_sums = jnp.sum(sums2_in[...], axis=(0, 2))
+    all_sums = jnp.sum(sums2_in[...], axis=0)
     all_sums = group_total(jnp.concatenate([all_sums, jnp.zeros((6, 128), f32)], axis=0)) / members
     mean_grad, mean_cross = all_sums[0:1], all_sums[1:2]
 
@@ -464,7 +468,9 @@
 
 def store(*refs):
     sources, targets, sems = refs[0:4], refs[4:8], refs[8]
-    copies = [pltpu.make_async_copy(sources[k], targets[k], sems.at[k]) for k in range(4)]
+    pairs = [(sources[k].at[f], targets[k].at[f]) for k in range(2) for f in range(4)]
+    pairs += [(sources[k], targets[k]) for k in range(2, 4)]
+    copies = [pltpu.make_async_copy(source, target, sems.at[k]) for k, (source, target) in enumerate(pairs)]
     for copy in copies:
         copy.start()
     for copy in copies:
@@ -499,10 +505,10 @@
             pltpu.VMEM((2, 384, 128), bf16),
             pltpu.VMEM((2, 384, 128), bf16),
             pltpu.VMEM((256, 1536), bf16),
-            pltpu.VMEM((2, 8, 128), f32),
-            pltpu.VMEM((n_ctx, 2, 8, 128), f32),
-            pltpu.VMEM((2, 8, 128), f32),
-            pltpu.VMEM((n_ctx, 2, 8, 128), f32),
+            pltpu.VMEM((2, 128), f32),
+            pltpu.VMEM((n_ctx, 2, 128), f32),
+            pltpu.VMEM((2, 128), f32),
+            pltpu.VMEM((n_ctx, 2, 128), f32),
             pltpu.VMEM((3, n_ctx, 2, 16, 1280), f32),
             pltpu.VMEM((3, n_ctx, 16, 1280), f32),
             pltpu.VMEM((128, 3584), f32),
@@ -518,7 +524,7 @@
             pltpu.VMEM((4, 384, 128), bf16),
             pltpu.VMEM((32, 108), f32),
             pltpu.VMEM((4, 32), f32),
-            dma((6,)), dma((2,)), dma((2,)),
+            dma((7,)), dma((2,)), dma((2,)),
             dma((n_ctx,)), dma((n_ctx,)), dma((n_ctx,)), dma((n_ctx,)),
             dma((3,)), dma((3,)), dma((4, 2, 4)), dma((4, 2, 4)), dma((4, 2, 4)), dma((4, 2, 4)),
             dma((4, 2, 2)), dma((8, 2)), dma((10,)),
@@ -538,7 +544,7 @@
         out_shape=shapes,
         in_specs=[anywhere] * 4,
         out_specs=(anywhere,) * 4,
-        scratch_shapes=[dma((4,))],
+        scratch_shapes=[dma((10,))],
         name="store",
     )(*[pltpu.with_memory_space_constraint(value, pltpu.VMEM) for value in results])
     return out.reshape(1, 4, 4, 96, 256), grad.reshape(1, 4, 4, 96, 128), conv.T, short

time: 41.1 us -> 40.2 us (0.978)
  Pallas kernels: 40.3 us -> 39.5 us
    pallas_call x1, Pallas kernels: 39.3 us -> 38.4 us  [body(): pl.pallas_call(functools.partial(kernel, n_dp, n_ctx), out_shape=shapes,...]
where the time goes in v4:
time: 40.2 us; the launch traced here: 40.1 us
  Pallas kernels  39.5 us (98%)
  between operations  0.64 us (2%)
    pallas_call x1, Pallas kernels, body(): pl.pallas_call(functools.partial(kernel, n_dp, n_ctx), out_shape=shapes,...  38.4 us
    pallas_call x1, Pallas kernels, body(): pl.pallas_call(store, out_shape=shapes, in_specs=[anywhere] * 4, out_spec...  1.09 us

profile of v4, /device:TPU:1, one launch (start us, length us, event | category | flops | bytes accessed | tf_op | source)
XLA Modules:
  0.0 40.1 jit_solution(11570087617506514536)
XLA Ops:
  0.6 38.4 %conv_block.1 = (bf16[4,384,256]{2,1,0:T(8,128)(2,1)S(1)}, bf16[4,384,128]{2,1,0:T(8,128)(2,1)S(1)}, f32[32,108]{1,0:T(8,128)S(1)}, f32[4,32]{1,0:T(4,128)S(1)}) custom-call(bf16[4,384,128]{2,1,0:T(8,128)(2,1)} %bitcast.8, bf16[4,384,256]{2,1,0:T(8,128)(2,1)} %bitcast.7, f32[1,128]{1,0:T(1,128)} %bitcast.9, f32[1,128]{1,0:T(1,128)} %bitcast.10, ...), custom_call_target="tpu_custom_call" | custom-call | tf_op jit(solution)/shard_map/conv_block/pallas_call | solution.py:491
  39.0 1.1 %store.1 = (bf16[4,384,256]{2,1,0:T(8,128)(2,1)}, bf16[4,384,128]{2,1,0:T(8,128)(2,1)}, f32[32,108]{1,0:T(8,128)}, f32[4,32]{1,0:T(4,128)}) custom-call(bf16[4,384,256]{2,1,0:T(8,128)(2,1)S(1)} %get-tuple-element.12.refs_0_, bf16[4,384,128]{2,1,0:T(8,128)(2,1)S(1)} %get-tuple-element.13.refs_1_, f32[32,108]{1,0:T(8,128)S(1)} %get-tuple-element.14.refs_2_, ...), custom_call_target="tpu_custom_call" | custom-call | tf_op jit(solution)/shard_map/store/pallas_call | solution.py:542

commit v5 on v4

--- a/solution.py
+++ b/solution.py
@@ -170,8 +170,6 @@
     @pl.when(ctx > 0)
     def _():
         edge_halo.start()
-
-    back[1] = back_terms(1, (0, 1, 2))
 
     each_ctx(lambda peer: sums_arrival(sums, sums_in, s_send, s_recv, peer).wait_recv())
     all_sums = jnp.sum(sums_in[...], axis=0)
@@ -344,6 +342,7 @@
     begin(0)
 
     back[3] = back_terms(3, (2,))
+    back[1] = back_terms(1, (0, 1, 2))
 
     @pl.when(ctx < n_ctx - 1)
     def _():
@@ -439,13 +438,10 @@
                 def _():
                     third_step(quarter, to_lo, to_core).wait_send()
 
-    for from_z in range(8):
-        for from_core in range(2):
-            mine = (z_hi * 2 + z_lo == from_z) & (core == from_core)
-
-            @pl.when(jnp.logical_not(mine))
-            def _():
-                third_arrival(from_z, from_core).wait_recv()
+    place = (z_hi * 2 + z_lo) * 2 + core
+    for k in range(1, 16):
+        source = (place + k) % 16
+        third_arrival(source // 2, source % 2).wait_recv()
 
     halves = []
     for h in range(2):

time: 40.2 us -> 40.2 us (level)
  no operation moved by 1% of the time
where the time goes in v5:
time: 40.2 us; the launch traced here: 40.1 us
  Pallas kernels  39.5 us (98%)
  between operations  0.64 us (2%)
    pallas_call x1, Pallas kernels, body(): pl.pallas_call(functools.partial(kernel, n_dp, n_ctx), out_shape=shapes,...  38.4 us
    pallas_call x1, Pallas kernels, body(): pl.pallas_call(store, out_shape=shapes, in_specs=[anywhere] * 4, out_spec...  1.09 us

profile of v5, /device:TPU:1, one launch (start us, length us, event | category | flops | bytes accessed | tf_op | source)
XLA Modules:
  0.0 40.1 jit_solution(10551863735458671654)
XLA Ops:
  0.6 38.4 %conv_block.1 = (bf16[4,384,256]{2,1,0:T(8,128)(2,1)S(1)}, bf16[4,384,128]{2,1,0:T(8,128)(2,1)S(1)}, f32[32,108]{1,0:T(8,128)S(1)}, f32[4,32]{1,0:T(4,128)S(1)}) custom-call(bf16[4,384,128]{2,1,0:T(8,128)(2,1)} %bitcast.8, bf16[4,384,256]{2,1,0:T(8,128)(2,1)} %bitcast.7, f32[1,128]{1,0:T(1,128)} %bitcast.9, f32[1,128]{1,0:T(1,128)} %bitcast.10, ...), custom_call_target="tpu_custom_call" | custom-call | tf_op jit(solution)/shard_map/conv_block/pallas_call | solution.py:487
  39.0 1.1 %store.1 = (bf16[4,384,256]{2,1,0:T(8,128)(2,1)}, bf16[4,384,128]{2,1,0:T(8,128)(2,1)}, f32[32,108]{1,0:T(8,128)}, f32[4,32]{1,0:T(4,128)}) custom-call(bf16[4,384,256]{2,1,0:T(8,128)(2,1)S(1)} %get-tuple-element.12.refs_0_, bf16[4,384,128]{2,1,0:T(8,128)(2,1)S(1)} %get-tuple-element.13.refs_1_, f32[32,108]{1,0:T(8,128)S(1)} %get-tuple-element.14.refs_2_, ...), custom_call_target="tpu_custom_call" | custom-call | tf_op jit(solution)/shard_map/store/pallas_call | solution.py:538
